TPU v7x, 256 devices: a whole 4x4x8 slice. The times are simulated.
256 devices in a mesh: row: 8 (over y_lo, x), col: 32 (over z, y_hi, core).
Axes of the slice: x: 4, y: 4 (y_hi: 2, y_lo: 2; y = y_hi * 2 + y_lo), z: 8, core: 2. Of those that a mesh axis runs over, the one named last changes fastest.
Arguments:
- tile_counts: int32 [8, 32, 160, 128, 128], P('row', 'col'), may hold values from 0 to 1536, as said below
- tile_rows: int32 [8, 32, 160], P('row', 'col'), may hold values from 0 to 127, as said below
- tile_cols: int32 [8, 32, 160], P('row', 'col'), may hold values from 0 to 31
- panel: bfloat16 [131072, 128], P(('col', 'row')), may hold values from -0.059814453 to 0.059814453
Outputs:
- word_panel: float32 [131072, 128], P(('row', 'col'))
- context_panel: float32 [131072, 128], P(('col', 'row'))
Inputs may be any that keep to these rules, and one draw needn't show every extreme that they name: `tile_counts`: on each device the occupied tiles come first: every slot at or after that device's number of occupied tiles holds only zeros, and some device has all 160 slots occupied. On each device the pairs (tile_rows, tile_cols) of the slots are distinct.
All inputs are finite; a program needn't handle non-finite values.
Results may differ from a plain program's by a relative error of at most 0.0029.
Values may be sent and summed in bfloat16 or wider, within the bound.
A program may use at most 128 MiB of HBM per device.

v0:
```python
import math

import jax
import jax.numpy as jnp
from jax import lax
from jax.sharding import Mesh
from jax.sharding import PartitionSpec as P

VOCAB = 131072
NEG_SAMPLES = 15
COL = ("col_0", "col_1", "col_2")
COL_ROW = ("col_0", "col_1", "col_2", "row")
ROW_COL = ("row", "col_0", "col_1", "col_2")


def laid_out(parts, dim):
    shape = list(parts.shape[1:])
    shape[dim] *= parts.shape[0]
    return jnp.moveaxis(parts, 0, dim).reshape(shape)


def from_everyone(x, axis):
    count = lax.axis_size(axis)
    return lax.all_to_all(jnp.broadcast_to(x[None], (count, *x.shape)), axis, 0, 0, tiled=True)


def collect(x, axis, dim):
    return laid_out(from_everyone(x, axis), dim)


def of_everyone(x, axis):
    return from_everyone(x, axis).sum(axis=0)


def together(arrays, axis):
    vector, at, outs = (jnp.concatenate([a.reshape(-1) for a in arrays]), 0, [])
    so_far = of_everyone(vector, axis)
    for a in arrays:
        outs.append(so_far[at : at + a.size].reshape(a.shape))
        at += a.size
    return tuple(outs)


def gather_in_order(x, axes, order):
    parts = x
    for k in order:
        parts = lax.all_gather(parts, axes[k])
    done = order[::-1]
    back = [done.index(k) for k in range(len(axes))]
    parts = parts.transpose(*back, *range(len(axes), parts.ndim))
    return parts.reshape(-1, *x.shape)


def gathered_by_axis(x, axes, order, dim):
    return laid_out(gather_in_order(x, axes, order), dim)


def in_blocks(x, dim, count):
    before, after = (x.shape[:dim], x.shape[dim + 1 :])
    return jnp.moveaxis(x.reshape(*before, count, -1, *after), dim, 0)


def sent_and_summed(x, axis, dim):
    parts = in_blocks(x, dim, lax.axis_size(axis))
    arrived = lax.all_to_all(parts, axis, split_axis=0, concat_axis=0, tiled=True)
    return arrived.sum(axis=0)


def ppmi_tiles(counts, word_rows, context_cols, row_totals, context_powers, log_scale):
    counts_float = counts.astype(jnp.float32)
    word_log = jnp.log(jnp.maximum(row_totals[word_rows], 1.0))
    context_log = jnp.log(jnp.maximum(context_powers[context_cols], 1.0))
    pointwise = (
        jnp.log(jnp.maximum(counts_float, 1.0))
        + log_scale
        - word_log[:, :, None]
        - context_log[:, None, :]
    )
    return jnp.where(counts > 0, jnp.maximum(pointwise, 0.0), 0.0).astype(jnp.bfloat16)


def shards(tile_counts, tile_rows, tile_cols, panel):
    counts = tile_counts[0, 0]
    word_rows = tile_rows[0, 0]
    context_cols = tile_cols[0, 0]
    tile_size = counts.shape[-1]
    panel_width = panel.shape[-1]
    band_rows = VOCAB // (tile_size * lax.axis_size("row"))
    panel_band = collect(panel, "row", 0)
    band_cols = panel_band.shape[0] // tile_size
    word_part = jax.ops.segment_sum(
        jnp.sum(counts, axis=2).astype(jnp.float32), word_rows, num_segments=band_rows
    )
    context_part = jax.ops.segment_sum(
        jnp.sum(counts, axis=1).astype(jnp.float32), context_cols, num_segments=band_cols
    )
    context_totals = of_everyone(context_part, "row")
    context_powers = context_totals**0.75
    band_power = jnp.sum(context_powers)
    row_totals, total_power = together((word_part, band_power), COL)
    log_scale = jnp.log(total_power) - math.log(NEG_SAMPLES)
    tiles = ppmi_tiles(counts, word_rows, context_cols, row_totals, context_powers, log_scale)
    picked = panel_band.reshape(band_cols, tile_size, panel_width)[context_cols]
    product = jnp.einsum("nij,njk->nik", tiles, picked, preferred_element_type=jnp.float32)
    word_partial = jax.ops.segment_sum(product, word_rows, num_segments=band_rows)
    word_partial = word_partial.reshape(band_rows * tile_size, panel_width)
    word_share = lax.psum_scatter(word_partial, COL, scatter_dimension=0, tiled=True)
    word_rounded = gathered_by_axis(word_share.astype(jnp.bfloat16), COL, (1, 0, 2), 0)
    word_picked = word_rounded.reshape(band_rows, tile_size, panel_width)[word_rows]
    context_product = jnp.einsum(
        "nji,njk->nik", tiles, word_picked, preferred_element_type=jnp.float32
    )
    context_partial = jax.ops.segment_sum(context_product, context_cols, num_segments=band_cols)
    context_partial = context_partial.reshape(band_cols * tile_size, panel_width)
    context_share = sent_and_summed(context_partial, "row", 0) / tile_size
    return (word_share, context_share)


def solution(mesh):
    split = Mesh(
        mesh.devices.reshape(mesh.shape["row"], 8, 2, 2), ("row", "col_0", "col_1", "col_2")
    )
    in_specs = (
        P("row", COL, None, None, None),
        P("row", COL, None),
        P("row", COL, None),
        P(COL_ROW, None),
    )
    out_specs = (P(ROW_COL, None), P(COL_ROW, None))
    return jax.shard_map(
        shards, mesh=split, in_specs=in_specs, out_specs=out_specs, check_vma=False
    )
```

profile of v0, /device:TPU:8, one launch (start us, length us, event | category | flops | bytes accessed | tf_op | source)
XLA Modules:
  0.0 473.4 jit_solution(3088928035881110731)
XLA Ops:
  7.2 6.8 %fusion.15 = (s32[160,128]{1,0:T(8,128)S(1)}, s32[160,128]{1,0:T(8,128)S(1)}) fusion(s32[1,1,160,128,128]{4,3,2,1,0:T(8,128)} %param.4), kind=kLoop, calls=%fused_computation.32 | loop fusion | flops 5201920 | bytes 10649600 | tf_op jit(solution)/shard_map/reduce_sum | solution.py:92
  14.0 1.1 scatter_custom_fusion.1
  15.2 10.7 %all_to_all.21 = f32[8,32,128]{2,1,0:T(8,128)S(1)} all-to-all(f32[8,32,128]{2,1,0:T(8,128)S(1)} %broadcast_in_dim.18), channel_id=1, replica_groups=mesh['row'=8,'col_0'=8,'col_1'=2,'col_2'=2] {'row'}, dimensions={0} | all-to-all | bytes 262144 | tf_op jit(solution)/shard_map/all_to_all | solution.py:24
  25.8 1.1 broadcast_in_dim.20
  27.0 4.9 %all-to-all-start.2 = ((bf16[8,512,128]{2,1,0:T(8,128)(2,1)}), bf16[8,512,128]{2,1,0:T(8,128)(2,1)S(1)}, u32[]{:S(2)}, u32[]{:S(2)}) async-start(bf16[8,512,128]{2,1,0:T(8,128)(2,1)} %broadcast_in_dim.20), calls=%async_computation.2 | async-start | bytes 2097152 | tf_op jit(solution)/shard_map/all_to_all | solution.py:24
  31.9 1.1 scatter_custom_fusion
  33.1 0.6 fusion.10
  33.7 0.7 pad_maximum_fusion
  34.4 10.7 %all-to-all-done.2 = bf16[8,512,128]{2,1,0:T(8,128)(2,1)S(1)} async-done(((bf16[8,512,128]{2,1,0:T(8,128)(2,1)}), bf16[8,512,128]{2,1,0:T(8,128)(2,1)S(1)}, u32[]{:S(2)}, u32[]{:S(2)}) %all-to-all-start.2) | async-done | bytes 1048608 | tf_op jit(solution)/shard_map/all_to_all | solution.py:24
  45.0 2.4 broadcast_in_dim.19
  47.5 10.6 %all-to-all-start.1 = ((f32[32,1,16385]{2,1,0:T(1,128)}), f32[32,1,16385]{2,1,0:T(1,128)S(1)}, u32[]{:S(2)}, u32[]{:S(2)}) async-start(f32[32,1,16385]{2,1,0:T(1,128)} %broadcast_in_dim.19), calls=%async_computation.1 | async-start | bytes 4227072 | tf_op jit(solution)/shard_map/all_to_all | solution.py:24
  58.3 0.7 gather_fusion.1
  59.0 7.8 %gather_fusion.2 = bf16[160,128,128]{2,1,0:T(8,128)(2,1)} fusion(bf16[32,128,128]{2,1,0:T(8,128)(2,1)S(1)} %bitcast.42, s32[1024]{0:T(1024)S(1)} %pad_clamp_fusion), kind=kCustom, calls=%fused_computation.2 | custom fusion | bytes 10486400 | tf_op jit(solution)/shard_map/gather | solution.py:103
  66.8 42.0 %all-to-all-done.1 = f32[32,1,16385]{2,1,0:T(1,128)S(1)} async-done(((f32[32,1,16385]{2,1,0:T(1,128)}), f32[32,1,16385]{2,1,0:T(1,128)S(1)}, u32[]{:S(2)}, u32[]{:S(2)}) %all-to-all-start.1) | async-done | bytes 2097312 | tf_op jit(solution)/shard_map/all_to_all | solution.py:24
  108.7 1.2 reduce_sum.58
  109.9 0.5 slice.16
  111.2 0.7 gather_fusion
  111.9 13.3 %fusion.13 = f32[160,128,128]{2,1,0:T(8,128)} fusion(bf16[160,128,128]{2,1,0:T(8,128)(2,1)} %gather_fusion.2, s32[1,1,160,128,128]{4,3,2,1,0:T(8,128)} %param.4, f32[160,128]{1,0:T(8,128)S(1)} %get-tuple-element.6, f32[160,128]{1,0:T(8,128)S(1)} %get-tuple-element.7, f32[]{:T(128)} %bitcast.5), kind=kOutput, calls=%fused_computation.31 | convolution fusion | flops 694681600 | bytes 26378244 | tf_op jit(solution)/shard_map/nij,njk->nik/dot_general | solution.py:104
  125.2 4.4 broadcast_in_dim.15
  129.6 33.1 %scatter_fusion = f32[128,128,128]{2,1,0:T(8,128)} fusion(f32[128,128,128]{2,1,0:T(8,128)} %broadcast_in_dim.15, s32[160]{0:T(256)S(1)} %bitcast.49, f32[160,128,128]{2,1,0:T(8,128)} %fusion.13), kind=kCustom, calls=%fused_computation.6 | custom fusion | flops 2621440 | bytes 31457920 | tf_op jit(solution)/shard_map/scatter-add | solution.py:105
  162.8 150.9 %reduce-scatter.2.cloned.1.call-done = f32[512,128]{1,0:T(8,128)} async-done(((f32[16384,128]{1,0:T(8,128)}), f32[512,128]{1,0:T(8,128)}) %reduce-scatter.2.cloned.1.call-update) | async-done | bytes 262160 | tf_op jit(solution)/shard_map/reduce_scatter | solution.py:107
  313.7 1.0 convert_element_type.20
  314.7 7.2 %all-gather = bf16[1024,128]{1,0:T(8,128)(2,1)} all-gather(bf16[512,128]{1,0:T(8,128)(2,1)S(1)} %convert_element_type.20), channel_id=2, replica_groups=mesh['row'=8,'col_0'=8,'col_1'=2,'col_2'=2] {'col_1'}, dimensions={0}, use_global_device_ids=true | all-gather | bytes 393216 | tf_op jit(solution)/shard_map/all_gather | solution.py:47
  322.2 39.8 %all-gather.6.cloned.1.call-done = bf16[16,512,128]{2,1,0:T(8,128)(2,1)} async-done(((bf16[2,512,128]{2,1,0:T(8,128)(2,1)}), bf16[16,512,128]{2,1,0:T(8,128)(2,1)}) %all-gather.6.cloned.1.call-update) | async-done | bytes 2097168 | tf_op jit(solution)/shard_map/all_gather | solution.py:47
  362.0 19.4 %all-gather.8.cloned.1.call-done = bf16[16,2,512,128]{3,2,1,0:T(8,128)(2,1)} async-done(((bf16[8,2,512,128]{3,2,1,0:T(8,128)(2,1)}), bf16[16,2,512,128]{3,2,1,0:T(8,128)(2,1)}) %all-gather.8.cloned.1.call-update) | async-done | bytes 4194320 | tf_op jit(solution)/shard_map/all_gather | solution.py:47
  381.4 4.6 copy.15
  386.0 10.0 %gather_fusion.3 = bf16[160,128,128]{2,1,0:T(8,128)(2,1)} fusion(bf16[128,128,128]{2,1,0:T(8,128)(2,1)} %bitcast.43, s32[1024]{0:T(1024)S(1)} %pad_clamp_fusion.1), kind=kCustom, calls=%fused_computation.3 | custom fusion | bytes 10486400 | tf_op jit(solution)/shard_map/gather | solution.py:109
  395.9 15.5 %fusion.11 = f32[160,128,128]{2,1,0:T(8,128)} fusion(bf16[160,128,128]{2,1,0:T(8,128)(2,1)} %gather_fusion.3, s32[1,1,160,128,128]{4,3,2,1,0:T(8,128)} %param.4, f32[160,128]{1,0:T(8,128)S(1)} %get-tuple-element.6, f32[160,128]{1,0:T(8,128)S(1)} %get-tuple-element.7, f32[]{:T(128)} %bitcast.5), kind=kOutput, calls=%fused_computation.30 | convolution fusion | flops 694681600 | bytes 26378244 | tf_op jit(solution)/shard_map/nji,njk->nik/dot_general | solution.py:110
  411.7 21.2 %scatter_fusion.1 = f32[32,128,128]{2,1,0:T(8,128)S(1)} fusion(f32[32,128,128]{2,1,0:T(8,128)S(1)} %broadcast_in_dim.22, s32[160]{0:T(256)S(1)} %bitcast.51, f32[160,128,128]{2,1,0:T(8,128)} %fusion.11), kind=kCustom, calls=%fused_computation.7 | custom fusion | flops 2621440 | bytes 31457920 | tf_op jit(solution)/shard_map/scatter-add | solution.py:113
  432.9 31.5 %all_to_all.22 = f32[8,512,128]{2,1,0:T(8,128)} all-to-all(f32[8,512,128]{2,1,0:T(8,128)S(1)} %bitcast.40), channel_id=1, replica_groups=mesh['row'=8,'col_0'=8,'col_1'=2,'col_2'=2] {'row'}, dimensions={0} | all-to-all | bytes 4194304 | tf_op jit(solution)/shard_map/all_to_all | solution.py:65
  464.4 1.7 reduce_sum.59
  466.2 0.7 broadcast_multiply_fusion
  (21 shorter events, 0.9 us)
Async XLA Ops:
  7.2 6.8 %copy-start.2 = (s32[1,1,160]{2,1,0:T(1,128)S(1)}, s32[1,1,160]{2,1,0:T(1,128)}, u32[]{:S(2)}) copy-start(s32[1,1,160]{2,1,0:T(1,128)} %param.6) | copy-start | bytes 1924
  7.2 18.7 %copy-start = (bf16[512,128]{1,0:T(8,128)(2,1)S(1)}, bf16[512,128]{1,0:T(8,128)(2,1)}, u32[]{:S(2)}) copy-start(bf16[512,128]{1,0:T(8,128)(2,1)} %param.7) | copy-start | bytes 393220
  7.2 24.7 %copy-start.1 = (s32[1,1,160]{2,1,0:T(1,128)S(1)}, s32[1,1,160]{2,1,0:T(1,128)}, u32[]{:S(2)}) copy-start(s32[1,1,160]{2,1,0:T(1,128)} %param.5) | copy-start | bytes 1924
  27.0 18.1 %all-to-all-start.2 = ((bf16[8,512,128]{2,1,0:T(8,128)(2,1)}), bf16[8,512,128]{2,1,0:T(8,128)(2,1)S(1)}, u32[]{:S(2)}, u32[]{:S(2)}) async-start(bf16[8,512,128]{2,1,0:T(8,128)(2,1)} %broadcast_in_dim.20), calls=%async_computation.2 | async-start | bytes 2097152 | tf_op jit(solution)/shard_map/all_to_all | solution.py:24
  47.5 61.3 %all-to-all-start.1 = ((f32[32,1,16385]{2,1,0:T(1,128)}), f32[32,1,16385]{2,1,0:T(1,128)S(1)}, u32[]{:S(2)}, u32[]{:S(2)}) async-start(f32[32,1,16385]{2,1,0:T(1,128)} %broadcast_in_dim.19), calls=%async_computation.1 | async-start | bytes 4227072 | tf_op jit(solution)/shard_map/all_to_all | solution.py:24
  58.1 255.6 %reduce-scatter.2.cloned.1.call-start = ((), (), s32[]{:S(2)}) async-start(), calls=%async_computation.5 | async-start | bytes 8650752 | tf_op jit(solution)/shard_map/reduce_scatter | solution.py:107
  162.7 199.2 %all-gather.6.cloned.1.call-start = ((), (), s32[]{:S(2)}) async-start(), calls=%async_computation.6 | async-start | bytes 2359296 | tf_op jit(solution)/shard_map/all_gather | solution.py:47
  321.9 59.4 %all-gather.8.cloned.1.call-start = ((), (), s32[]{:S(2)}) async-start(), calls=%async_computation.7 | async-start | bytes 6291456 | tf_op jit(solution)/shard_map/all_gather | solution.py:47
Sparse Core Ops, SparseCore 0:
  162.9 150.7 reduce-scatter.1
  322.1 39.8 all-gather.5
  363.8 17.5 all-gather.7
where the time goes:
time: 476 us; the launch traced here: 473 us
  waiting for transfers between devices  263 us (55%)
  other arithmetic  69.3 us (15%)
  blocking collectives  49.5 us (10%)
  local copies, waits for them, and re-layouts  32.4 us (7%)
  matrix products  28.8 us (6%)
  starting transfers between devices  16.1 us (3%)
  between operations  14.6 us (3%)
    reduce_scatter x1, waiting for transfers between devices, shards(): lax.psum_scatter(word_partial, COL, scatter_dimension=0, tiled=True)  151 us
    all_gather x2, waiting for transfers between devices, gather_in_order(): parts = lax.all_gather(parts, axes[k])  59.2 us
    all_to_all x2, waiting for transfers between devices, from_everyone(): lax.all_to_all(jnp.broadcast_to(x[None], (count, *x.shape)), axis, 0, 0,...  52.6 us
    scatter-add x1, other arithmetic, shards(): jax.ops.segment_sum(product, word_rows, num_segments=band_rows)  33.1 us
    all_to_all x1, blocking collectives, sent_and_summed(): lax.all_to_all(parts, axis, split_axis=0, concat_axis=0, tiled=True)  31.5 us
    scatter-add x1, other arithmetic, shards(): jax.ops.segment_sum(context_product, context_cols, num_segments=band_cols)  21.2 us
    dot_general x1, matrix products, shards(): jnp.einsum('nji,njk->nik', tiles, word_picked, preferred_element_type=jnp...  15.5 us
    all_to_all x2, starting transfers between devices, from_everyone(): lax.all_to_all(jnp.broadcast_to(x[None], (count, *x.shape)), axis, 0, 0,...  15.5 us
  transfers between devices with their start and end apart: 5, of which 5 were waited for; matrix products, arithmetic and copies ran while one was open for 2% of the time, Pallas kernels for 0%

commit v1 on v0

v1 whole, which is shorter than its diff:
```python
import functools
import math

import jax
import jax.numpy as jnp
from jax import lax
from jax.experimental import pallas as pl
from jax.experimental.pallas import tpu as pltpu
from jax.sharding import Mesh
from jax.sharding import PartitionSpec as P

NEG_SAMPLES = 15
T = 128
NX, NYL, NYH, NZ, NC = 4, 2, 2, 8, 2
N_ROW, N_COL = NX * NYL, NZ * NYH * NC
ROW_TILES, COL_TILES = 128, 32
SHARE = 512
CODE = SHARE + 16
MESH = pl.DeviceIdType.MESH
F32, BF16, I32, I16 = jnp.float32, jnp.bfloat16, jnp.int32, jnp.int16
ANY = pl.BlockSpec(memory_space=pl.ANY)
VMEM = pl.BlockSpec(memory_space=pltpu.VMEM)
DMA = pltpu.SemaphoreType.DMA
LN2 = math.log(2.0)


def remote(src, dst, ssem, rsem, device):
    return pltpu.make_async_remote_copy(
        src_ref=src, dst_ref=dst, send_sem=ssem, recv_sem=rsem,
        device_id=device, device_id_type=MESH,
    )


def greet(devices):
    barrier = pltpu.get_barrier_semaphore()
    for device in devices:
        pl.semaphore_signal(barrier, inc=1, device_id=device, device_id_type=MESH)
    pl.semaphore_wait(barrier, len(devices))


def encode(value, ref):
    top = jnp.max(jnp.abs(value), axis=0, keepdims=True)
    expo = jnp.ceil(jnp.log(jnp.maximum(top, 1e-30)) * (1.0 / LN2) + 0.001) - 14.0
    scaled = jnp.round(value * jnp.exp(expo * -LN2))
    ref[pl.ds(0, SHARE), :] = scaled.astype(I32).astype(I16)
    ref[pl.ds(SHARE, 16), :] = jnp.broadcast_to(expo, (16, T)).astype(I32).astype(I16)


def decode(ref):
    expo = ref[pl.ds(SHARE, 16), :].astype(I32).astype(F32)[0:1]
    return ref[pl.ds(0, SHARE), :].astype(I32).astype(F32) * jnp.exp(expo * LN2)


def count_kernel(group, rows, cols, counts, words, contexts, wacc, cacc):
    step = pl.program_id(0)

    @pl.when(step == 0)
    def _():
        wacc[...] = jnp.zeros_like(wacc)
        cacc[...] = jnp.zeros_like(cacc)

    lanes = lax.broadcasted_iota(I32, (T, T), 1)
    total = wacc[...]
    for g in range(group):
        slot = step * group + g
        value = counts[g]
        cacc[pl.ds(cols[slot], 1), :] += jnp.sum(value, axis=0, keepdims=True)
        per_word = jnp.sum(value.astype(F32), axis=1, keepdims=True)
        total = total + jnp.where(lanes == rows[slot], per_word, 0.0)
    wacc[...] = total

    @pl.when(step == pl.num_programs(0) - 1)
    def _():
        contexts[...] = cacc[...].astype(F32)
        words[...] = jnp.zeros_like(words)
        for d in range(N_COL):
            words[d, 0:4, :] = wacc[pl.ds(4 * d, 4), :]


def count_sums(rows, cols, counts, group=16):
    slots = counts.shape[0]
    return pl.pallas_call(
        functools.partial(count_kernel, group),
        grid_spec=pltpu.PrefetchScalarGridSpec(
            num_scalar_prefetch=2,
            grid=(slots // group,),
            in_specs=[pl.BlockSpec((group, T, T), lambda i, r, c: (i, 0, 0))],
            out_specs=[
                pl.BlockSpec((N_COL, 8, T), lambda i, r, c: (0, 0, 0)),
                pl.BlockSpec((COL_TILES, T), lambda i, r, c: (0, 0)),
            ],
            scratch_shapes=[pltpu.VMEM((T, ROW_TILES), F32), pltpu.VMEM((COL_TILES, T), I32)],
        ),
        out_shape=[
            jax.ShapeDtypeStruct((N_COL, 8, T), F32),
            jax.ShapeDtypeStruct((COL_TILES, T), F32),
        ],
        name="count_sums",
    )(rows, cols, counts)


def powers_of(totals):
    root = jnp.sqrt(totals)
    return root * jnp.sqrt(root)


def totals_kernel(words, contexts, panel, words_all, contexts_all, band,
                  wrecv, crecv, mine, wss, wrs, css, crs, ass, ars, pss, prs, lsem):
    x, yl = lax.axis_index("x"), lax.axis_index("yl")
    z, yh, c = lax.axis_index("z"), lax.axis_index("yh"), lax.axis_index("core")
    row = yl * NX + x
    col = (z * NYH + yh) * NC + c
    row_peers = [
        (dx * NYL + dy, {"x": lax.rem(x + dx, NX), "yl": lax.rem(yl + dy, NYL)})
        for dx in range(NX) for dy in range(NYL) if dx or dy
    ]
    col_peers = []
    for dz in (4, 3, 5, 2, 6, 1, 7, 0):
        for dy in (1, 0):
            for dc in range(NC):
                if dz or dy or dc:
                    pz, py, pc = lax.rem(z + dz, NZ), lax.rem(yh + dy, NYH), lax.rem(c + dc, NC)
                    col_peers.append(
                        ((dz * NYH + dy) * NC + dc, (pz * NYH + py) * NC + pc,
                         {"z": pz, "yh": py, "core": pc})
                    )
    greet([d for _, d in row_peers] + [d for _, _, d in col_peers])

    waits = []
    csends = [remote(contexts, crecv.at[k], css.at[k], crs.at[k], d) for k, d in row_peers]
    wsends = [remote(words.at[p], wrecv.at[k], wss.at[k], wrs.at[k], d) for k, p, d in col_peers]
    psends = [remote(panel, band.at[row], pss.at[k], prs.at[k], d) for k, d in row_peers]
    own = pltpu.make_async_copy(panel, band.at[row], lsem.at[0])
    for copy in csends + wsends + psends:
        copy.start()
    own.start()

    for copy in csends:
        copy.wait_recv()
    contexts_sum = contexts[...]
    for k, _ in row_peers:
        contexts_sum = contexts_sum + crecv[k]
    contexts_all[...] = contexts_sum
    band_power = jnp.sum(powers_of(contexts_sum), keepdims=True)

    for copy in wsends:
        copy.wait_recv()
    words_sum = words[col]
    for k, _, _ in col_peers:
        words_sum = words_sum + wrecv[k]
    at = lax.broadcasted_iota(I32, (8, T), 0)
    mine[...] = jnp.where(at == 4, jnp.broadcast_to(band_power, (8, T)), words_sum)
    asends = [remote(mine, words_all.at[col], ass.at[k], ars.at[k], d) for k, _, d in col_peers]
    for copy in asends:
        copy.start()
    words_all[col] = mine[...]
    for copy in asends:
        copy.wait()
    for copy in csends + wsends:
        copy.wait_send()
    for copy in psends:
        copy.wait()
    own.wait()


def totals(words, contexts, panel):
    return pl.pallas_call(
        totals_kernel,
        in_specs=[VMEM, VMEM, ANY],
        out_specs=[VMEM, VMEM, ANY],
        out_shape=[
            jax.ShapeDtypeStruct((N_COL, 8, T), F32),
            jax.ShapeDtypeStruct((COL_TILES, T), F32),
            jax.ShapeDtypeStruct((N_ROW, SHARE, T), BF16),
        ],
        scratch_shapes=[
            pltpu.VMEM((N_COL, 8, T), F32),
            pltpu.VMEM((N_ROW, COL_TILES, T), F32),
            pltpu.VMEM((8, T), F32),
            DMA((N_COL,)), DMA((N_COL,)), DMA((N_ROW,)), DMA((N_ROW,)),
            DMA((N_COL,)), DMA((N_COL,)), DMA((N_ROW,)), DMA((N_ROW,)), DMA((1,)),
        ],
        compiler_params=pltpu.CompilerParams(collective_id=0, has_side_effects=True),
        name="totals",
    )(words, contexts, panel)


def word_kernel(group, rows, cols, counts, words_all, contexts_all, band, tiles, partial,
                word_term, context_log):
    step = pl.program_id(0)

    @pl.when(step == 0)
    def _():
        power = jnp.zeros((1, T), F32)
        for d in range(N_COL):
            word_term[pl.ds(4 * d, 4), :] = words_all[d, 0:4, :]
            power = power + words_all[d, 4:5, :]
        log_scale = jnp.log(power) - math.log(NEG_SAMPLES)
        word_term[...] = log_scale - jnp.log(jnp.maximum(word_term[...], 1.0))
        context_log[...] = jnp.log(jnp.maximum(powers_of(contexts_all[...]), 1.0))
        partial[...] = jnp.zeros_like(partial)

    lanes = lax.broadcasted_iota(I32, (T, T), 1)
    for g in range(group):
        slot = step * group + g
        row, col = rows[slot], cols[slot]
        value = counts[g]
        per_word = jnp.sum(jnp.where(lanes == row, word_term[...], 0.0), axis=1, keepdims=True)
        pointwise = jnp.log(value.astype(F32)) + per_word - context_log[pl.ds(col, 1), :]
        tile = jnp.where(value > 0, jnp.maximum(pointwise, 0.0), 0.0).astype(BF16)
        tiles[g] = tile
        partial[row] += jnp.dot(tile, band[col], preferred_element_type=F32)


def word_products(rows, cols, counts, words_all, contexts_all, band, group=16):
    slots = counts.shape[0]
    whole3 = lambda i, r, c: (0, 0, 0)
    return pl.pallas_call(
        functools.partial(word_kernel, group),
        grid_spec=pltpu.PrefetchScalarGridSpec(
            num_scalar_prefetch=2,
            grid=(slots // group,),
            in_specs=[
                pl.BlockSpec((group, T, T), lambda i, r, c: (i, 0, 0)),
                pl.BlockSpec((N_COL, 8, T), whole3),
                pl.BlockSpec((COL_TILES, T), lambda i, r, c: (0, 0)),
                pl.BlockSpec((COL_TILES, T, T), whole3),
            ],
            out_specs=[
                pl.BlockSpec((group, T, T), lambda i, r, c: (i, 0, 0)),
                pl.BlockSpec((ROW_TILES, T, T), whole3),
            ],
            scratch_shapes=[pltpu.VMEM((T, ROW_TILES), F32), pltpu.VMEM((COL_TILES, T), F32)],
        ),
        out_shape=[
            jax.ShapeDtypeStruct((slots, T, T), BF16),
            jax.ShapeDtypeStruct((ROW_TILES, T, T), F32),
        ],
        name="word_products",
    )(rows, cols, counts, words_all, contexts_all, band)


def chain_steps(length):
    steps = []
    for s in range(length):
        for way, half in ((0, 1), (1, 0), (0, 0), (1, 1)):
            if s > 0 or way == half:
                steps.append((s, way, half))
    return steps


Z_STEPS = chain_steps(NZ // 2)
X_STEPS = chain_steps(NX // 2)


def word_panel_kernel(partial, share, everyone, own, sib, sendb, recvb, ysend, yrecv, mine,
                      lsem, xss, xrs, zss, zrs, yss, yrs, gss, grs, hss, hrs, ms):
    z, yh, c = lax.axis_index("z"), lax.axis_index("yh"), lax.axis_index("core")
    ways = ({"z": lax.rem(z + 1, NZ)}, {"z": lax.rem(z + NZ - 1, NZ)})
    other_y, other_core = {"yh": 1 - yh}, {"core": 1 - c}

    loads, swaps = {}, {}
    order = [(dz, h) for dz in (4, 3, 5, 2, 6, 1, 7, 0) for h in range(2)]
    for dz, h in order:
        slot, zz = dz * 2 + h, lax.rem(z + dz, NZ)
        loads[dz, h] = pltpu.make_async_copy(partial.at[zz, h, c], own.at[slot], lsem.at[slot])
        loads[dz, h].start()
    greet([*ways, other_y, other_core])
    for dz, h in order:
        slot, zz = dz * 2 + h, lax.rem(z + dz, NZ)
        swaps[dz, h] = remote(partial.at[zz, h, 1 - c], sib.at[slot], xss.at[slot], xrs.at[slot], other_core)
        swaps[dz, h].start()

    def block(dz, h):
        loads[dz, h].wait()
        swaps[dz, h].wait_recv()
        return own[dz * 2 + h] + sib[dz * 2 + h]

    sends = {}
    for n, (s, way, half) in enumerate(Z_STEPS):
        value = block((NZ // 2 - s) if way == 0 else (NZ // 2 + s), half)
        if (s - 1, way, half) in sends:
            before = sends[s - 1, way, half]
            before[1].wait_recv()
            value = value + decode(recvb.at[before[0]])
        encode(value, sendb.at[n])
        copy = remote(sendb.at[n], recvb.at[n], zss.at[n], zrs.at[n], ways[way])
        copy.start()
        sends[s, way, half] = (n, copy)

    last = NZ // 2 - 1
    for h in range(2):
        loads[0, h].wait()
        swaps[0, h].wait_recv()
        for way in range(2):
            sends[last, way, h][1].wait_recv()

    def arrived(h):
        value = own[h] + sib[h]
        for way in range(2):
            first, second = sends[last, way, 0][0], sends[last, way, 1][0]
            value = value + decode(recvb.at[first + h * (second - first)])
        return value

    encode(arrived(1 - yh), ysend)
    ycopy = remote(ysend, yrecv, yss.at[0], yrs.at[0], other_y)
    ycopy.start()
    kept = arrived(yh)
    ycopy.wait_recv()
    total = kept + decode(yrecv)
    share[...] = total
    for t in range(4):
        mine[t] = total[t * T : (t + 1) * T].T.astype(BF16)

    halves = (yh, 1 - yh)
    home = everyone.at[z, yh, c]
    keep = pltpu.make_async_copy(mine, home, ms.at[0])
    keep.start()
    ygive = remote(mine, home, yss.at[1], yrs.at[1], other_y)
    ygive.start()
    gives, hands = {}, []

    def hand(src, place, k):
        copy = remote(src, place, hss.at[k], hrs.at[k], other_core)
        copy.start()
        hands.append(copy)

    def give(s, way, r, src):
        zz = lax.rem(z + (NZ - s if way == 0 else s), NZ)
        place = everyone.at[zz, halves[r], c]
        k = (s * 2 + way) * 2 + r
        copy = remote(place if src is None else src, place, gss.at[k], grs.at[k], ways[way])
        copy.start()
        gives[s, way, r] = copy

    give(0, 0, 0, mine)
    give(0, 1, 0, mine)
    hand(mine, home, 0)
    ygive.wait_recv()
    give(0, 0, 1, None)
    give(0, 1, 1, None)
    hand(everyone.at[z, 1 - yh, c], everyone.at[z, 1 - yh, c], 1)
    k = 2
    for s in range(1, NZ // 2 + 1):
        for r in range(2):
            for way in range(2):
                if (s - 1, way, r) not in gives:
                    continue
                gives[s - 1, way, r].wait_recv()
                if s < last or (s == last and way == r):
                    give(s, way, r, None)
                zz = lax.rem(z + (NZ - s if way == 0 else s), NZ)
                place = everyone.at[zz, halves[r], c]
                hand(place, place, k)
                k += 1

    for copy in hands:
        copy.wait()
    for copy in gives.values():
        copy.wait_send()
    for _, copy in sends.values():
        copy.wait_send()
    for copy in swaps.values():
        copy.wait_send()
    ycopy.wait_send()
    ygive.wait_send()
    keep.wait()


def word_panel_sum(partial):
    n = len(Z_STEPS)
    return pl.pallas_call(
        word_panel_kernel,
        in_specs=[ANY],
        out_specs=[VMEM, ANY],
        out_shape=[
            jax.ShapeDtypeStruct((SHARE, T), F32),
            jax.ShapeDtypeStruct((NZ, NYH, NC, 4, T, T), BF16),
        ],
        scratch_shapes=[
            pltpu.VMEM((2 * NZ, SHARE, T), F32),
            pltpu.VMEM((2 * NZ, SHARE, T), F32),
            pltpu.VMEM((n, CODE, T), I16),
            pltpu.VMEM((n, CODE, T), I16),
            pltpu.VMEM((CODE, T), I16),
            pltpu.VMEM((CODE, T), I16),
            pltpu.VMEM((4, T, T), BF16),
            DMA((2 * NZ,)), DMA((2 * NZ,)), DMA((2 * NZ,)), DMA((n,)), DMA((n,)),
            DMA((2,)), DMA((2,)), DMA((2 * NZ,)), DMA((2 * NZ,)),
            DMA((2 * NZ,)), DMA((2 * NZ,)), DMA((1,)),
        ],
        compiler_params=pltpu.CompilerParams(collective_id=1, has_side_effects=True),
        name="word_panel_sum",
    )(partial)


def context_kernel(group, rows, cols, tiles, rounded, partial):
    step = pl.program_id(0)

    @pl.when(step == 0)
    def _():
        partial[...] = jnp.zeros_like(partial)

    for g in range(group):
        slot = step * group + g
        partial[cols[slot]] += jnp.dot(rounded[rows[slot]], tiles[g], preferred_element_type=F32)


def context_products(rows, cols, tiles, rounded, group=16):
    slots = tiles.shape[0]
    whole3 = lambda i, r, c: (0, 0, 0)
    return pl.pallas_call(
        functools.partial(context_kernel, group),
        grid_spec=pltpu.PrefetchScalarGridSpec(
            num_scalar_prefetch=2,
            grid=(slots // group,),
            in_specs=[
                pl.BlockSpec((group, T, T), lambda i, r, c: (i, 0, 0)),
                pl.BlockSpec((ROW_TILES, T, T), whole3),
            ],
            out_specs=pl.BlockSpec((COL_TILES, T, T), whole3),
        ),
        out_shape=jax.ShapeDtypeStruct((COL_TILES, T, T), F32),
        name="context_products",
    )(rows, cols, tiles, rounded)


def context_panel_kernel(partial, share, sendb, recvb, ysend, yrecv, xss, xrs, yss, yrs):
    x, yl = lax.axis_index("x"), lax.axis_index("yl")
    ways = ({"x": lax.rem(x + 1, NX)}, {"x": lax.rem(x + NX - 1, NX)})
    other_y = {"yl": 1 - yl}
    greet([*ways, other_y])
    sends = {}
    for n, (s, way, half) in enumerate(X_STEPS):
        value = partial[half, lax.rem(x + (NX // 2 - s if way == 0 else NX // 2 + s), NX)]
        if (s - 1, way, half) in sends:
            before = sends[s - 1, way, half]
            before[1].wait_recv()
            value = value + decode(recvb.at[before[0]])
        encode(value, sendb.at[n])
        copy = remote(sendb.at[n], recvb.at[n], xss.at[n], xrs.at[n], ways[way])
        copy.start()
        sends[s, way, half] = (n, copy)
    last = NX // 2 - 1
    for h in range(2):
        for way in range(2):
            sends[last, way, h][1].wait_recv()

    def arrived(h):
        value = partial[h, x]
        for way in range(2):
            first, second = sends[last, way, 0][0], sends[last, way, 1][0]
            value = value + decode(recvb.at[first + h * (second - first)])
        return value

    encode(arrived(1 - yl), ysend)
    ycopy = remote(ysend, yrecv, yss.at[0], yrs.at[0], other_y)
    ycopy.start()
    kept = arrived(yl)
    ycopy.wait_recv()
    total = (kept + decode(yrecv)) * (1.0 / T)
    for t in range(4):
        share[pl.ds(t * T, T), :] = total[t * T : (t + 1) * T].T
    for _, copy in sends.values():
        copy.wait_send()
    ycopy.wait_send()


def context_panel_sum(partial):
    n = len(X_STEPS)
    return pl.pallas_call(
        context_panel_kernel,
        in_specs=[VMEM],
        out_specs=VMEM,
        out_shape=jax.ShapeDtypeStruct((SHARE, T), F32),
        scratch_shapes=[
            pltpu.VMEM((n, CODE, T), I16),
            pltpu.VMEM((n, CODE, T), I16),
            pltpu.VMEM((CODE, T), I16),
            pltpu.VMEM((CODE, T), I16),
            DMA((n,)), DMA((n,)), DMA((1,)), DMA((1,)),
        ],
        compiler_params=pltpu.CompilerParams(collective_id=2, has_side_effects=True),
        name="context_panel_sum",
    )(partial)


def shards(tile_counts, tile_rows, tile_cols, panel):
    counts, rows, cols = tile_counts[0, 0], tile_rows[0, 0], tile_cols[0, 0]
    words, contexts = count_sums(rows, cols, counts)
    words_all, contexts_all, band = totals(words, contexts, panel)
    band = band.reshape(COL_TILES, T, T)
    tiles, partial = word_products(rows, cols, counts, words_all, contexts_all, band)
    share, everyone = word_panel_sum(partial.reshape(NZ, NYH, NC, SHARE, T))
    rounded = everyone.reshape(ROW_TILES, T, T)
    context_partial = context_products(rows, cols, tiles, rounded)
    context_share = context_panel_sum(context_partial.reshape(NYL, NX, SHARE, T))
    return share, context_share


def solution(mesh):
    split = Mesh(
        mesh.devices.reshape(NYL, NX, NZ, NYH, NC), ("yl", "x", "z", "yh", "core")
    )
    row, col = ("yl", "x"), ("z", "yh", "core")
    in_specs = (
        P(row, col, None, None, None),
        P(row, col, None),
        P(row, col, None),
        P(col + row, None),
    )
    out_specs = (P(row + col, None), P(col + row, None))
    return jax.shard_map(shards, mesh=split, in_specs=in_specs, out_specs=out_specs, check_vma=False)
```

time: 476 us -> 153 us (0.32)
  waiting for transfers between devices: 263 us -> 0 us
  Pallas kernels: 0 us -> 149 us
  other arithmetic: 69.3 us -> 0 us
  blocking collectives: 49.5 us -> 0 us
  local copies, waits for them, and re-layouts: 32.4 us -> 2.38 us
  matrix products: 28.8 us -> 0 us
  starting transfers between devices: 16.1 us -> 0 us
  between operations: 14.6 us -> 0.67 us
    reduce_scatter x1 -> x0, waiting for transfers between devices: 151 us -> none  [shards(): lax.psum_scatter(word_partial, COL, scatter_dimension=0, tiled=True)]
    pallas_call x0 -> x6, Pallas kernels: none -> 149 us  [the longest x1 60.9 us: word_panel_sum(): pl.pallas_call(word_panel_kernel, in_specs=[ANY], out_specs=[VMEM, ANY],...]
    all_gather x2 -> x0, waiting for transfers between devices: 59.2 us -> none  [gather_in_order(): parts = lax.all_gather(parts, axes[k])]
    scatter-add x4 -> x0, other arithmetic: 56.6 us -> none  [the longest x1 33.1 us: shards(): jax.ops.segment_sum(product, word_rows, num_segments=band_rows)]
    all_to_all x2 -> x0, waiting for transfers between devices: 52.6 us -> none  [from_everyone(): lax.all_to_all(jnp.broadcast_to(x[None], (count, *x.shape)), axis, 0, 0,...]
    all_to_all x2 -> x0, blocking collectives: 42.2 us -> none  [the longest x1 31.5 us: sent_and_summed(): lax.all_to_all(parts, axis, split_axis=0, concat_axis=0, tiled=True)]
    dot_general x2 -> x0, matrix products: 28.8 us -> none  [the longest x1 15.5 us: shards(): jnp.einsum('nji,njk->nik', tiles, word_picked, preferred_element_type=jnp...]
    gather x4 -> x0, local copies, waits for them, and re-layouts: 19.1 us -> none  [the longest x1 9.95 us: shards(): word_rounded.reshape(band_rows, tile_size, panel_width)[word_rows]]
  transfers between devices with their start and end apart: 5 -> 0, of which waited for: 5 -> 0; matrix products, arithmetic and copies ran while one was open for 2% -> 0% of each run, Pallas kernels for 0% -> 0%
where the time goes in v1:
time: 153 us; the launch traced here: 152 us
  Pallas kernels  149 us (97%)
  local copies, waits for them, and re-layouts  2.38 us (2%)
    pallas_call x1, Pallas kernels, word_panel_sum(): pl.pallas_call(word_panel_kernel, in_specs=[ANY], out_specs=[VMEM, ANY],...  60.9 us
    pallas_call x1, Pallas kernels, totals(): pl.pallas_call(totals_kernel, in_specs=[VMEM, VMEM, ANY], out_specs=[VMEM...  30.7 us
    pallas_call x1, Pallas kernels, context_panel_sum(): pl.pallas_call(context_panel_kernel, in_specs=[VMEM], out_specs=VMEM, out...  21 us
    pallas_call x1, Pallas kernels, word_products(): pl.pallas_call(functools.partial(word_kernel, group), grid_spec=pltpu.Pre...  15.1 us
    pallas_call x1, Pallas kernels, context_products(): pl.pallas_call(functools.partial(context_kernel, group), grid_spec=pltpu....  10.9 us
    pallas_call x1, Pallas kernels, count_sums(): pl.pallas_call(functools.partial(count_kernel, group), grid_spec=pltpu.Pr...  9.97 us

profile of v1, /device:TPU:8, one launch (start us, length us, event | category | flops | bytes accessed | tf_op | source)
XLA Modules:
  0.0 151.6 jit_solution(8613978216474123954)
XLA Ops:
  0.6 10.0 %count_sums.1 = (f32[32,8,128]{2,1,0:T(8,128)}, f32[32,128]{1,0:T(8,128)}) custom-call(s32[160]{0:T(256)} %bitcast.13, s32[160]{0:T(256)} %bitcast.16, s32[160,128,128]{2,1,0:T(8,128)} %bitcast.7), custom_call_target="tpu_custom_call" | custom-call | tf_op jit(solution)/shard_map/count_sums/pallas_call | solution.py:82
  10.6 30.7 %totals.1 = (f32[32,8,128]{2,1,0:T(8,128)}, f32[32,128]{1,0:T(8,128)}, bf16[8,512,128]{2,1,0:T(8,128)(2,1)}) custom-call(f32[32,8,128]{2,1,0:T(8,128)} %get-tuple-element.11.words, f32[32,128]{1,0:T(8,128)} %get-tuple-element.12.contexts, bf16[512,128]{1,0:T(8,128)(2,1)} %panel.1), custom_call_target="tpu_custom_call" | custom-call | tf_op jit(solution)/shard_map/totals/pallas_call | solution.py:167
  41.3 15.1 %word_products.1 = (bf16[160,128,128]{2,1,0:T(8,128)(2,1)}, f32[128,128,128]{2,1,0:T(8,128)}) custom-call(s32[160]{0:T(256)} %bitcast.14, s32[160]{0:T(256)} %bitcast.17, s32[160,128,128]{2,1,0:T(8,128)} %bitcast.8, f32[32,8,128]{2,1,0:T(8,128)} %get-tuple-element.13.words_all, f32[32,128]{1,0:T(8,128)} %get-tuple-element.14.contexts_all, ...), custom_call_target="tpu_custom_call" | custom-call | tf_op jit(solution)/shard_map/word_products/pallas_call | solution.py:218
  56.4 60.9 %word_panel_sum.1 = (f32[512,128]{1,0:T(8,128)}, bf16[8,2,2,4,128,128]{5,4,3,2,1,0:T(8,128)(2,1)}) custom-call(f32[8,2,2,512,128]{4,3,2,1,0:T(8,128)} %bitcast.9), custom_call_target="tpu_custom_call" | custom-call | tf_op jit(solution)/shard_map/word_panel_sum/pallas_call | solution.py:372
  117.3 0.0 copy-start
  117.3 10.9 %context_products.1 = f32[32,128,128]{2,1,0:T(8,128)} custom-call(s32[160]{0:T(256)} %bitcast.15, s32[160]{0:T(256)} %bitcast.18, bf16[160,128,128]{2,1,0:T(8,128)(2,1)} %get-tuple-element.18.tiles, bf16[128,128,128]{2,1,0:T(8,128)(2,1)} %bitcast.11), custom_call_target="tpu_custom_call" | custom-call | tf_op jit(solution)/shard_map/context_products/pallas_call | solution.py:412
  128.2 21.0 %context_panel_sum.1 = f32[512,128]{1,0:T(8,128)} custom-call(f32[2,4,512,128]{3,2,1,0:T(8,128)} %bitcast.10), custom_call_target="tpu_custom_call" | custom-call | tf_op jit(solution)/shard_map/context_panel_sum/pallas_call | solution.py:471
  149.2 0.0 copy-done
  149.2 0.7 copy.8
  149.9 1.7 %copy.9 = f32[512,128]{1,0:T(8,128)} copy(f32[512,128]{1,0:T(8,128)} %context_panel_sum.1) | data formatting | bytes 524288
Async XLA Ops:
  117.3 31.9 %copy-start = (f32[512,128]{1,0:T(8,128)S(1)}, f32[512,128]{1,0:T(8,128)}, u32[]{:S(2)}) copy-start(f32[512,128]{1,0:T(8,128)} %get-tuple-element.22) | copy-start | bytes 786436

commit v2 on v1

--- a/solution.py
+++ b/solution.py
@@ -20,6 +20,7 @@
 F32, BF16, I32, I16 = jnp.float32, jnp.bfloat16, jnp.int32, jnp.int16
 ANY = pl.BlockSpec(memory_space=pl.ANY)
 VMEM = pl.BlockSpec(memory_space=pltpu.VMEM)
+SMEM = pl.BlockSpec(memory_space=pltpu.SMEM)
 DMA = pltpu.SemaphoreType.DMA
 LN2 = math.log(2.0)
 
@@ -51,52 +52,7 @@
     return ref[pl.ds(0, SHARE), :].astype(I32).astype(F32) * jnp.exp(expo * LN2)
 
 
-def count_kernel(group, rows, cols, counts, words, contexts, wacc, cacc):
-    step = pl.program_id(0)
-
-    @pl.when(step == 0)
-    def _():
-        wacc[...] = jnp.zeros_like(wacc)
-        cacc[...] = jnp.zeros_like(cacc)
-
-    lanes = lax.broadcasted_iota(I32, (T, T), 1)
-    total = wacc[...]
-    for g in range(group):
-        slot = step * group + g
-        value = counts[g]
-        cacc[pl.ds(cols[slot], 1), :] += jnp.sum(value, axis=0, keepdims=True)
-        per_word = jnp.sum(value.astype(F32), axis=1, keepdims=True)
-        total = total + jnp.where(lanes == rows[slot], per_word, 0.0)
-    wacc[...] = total
-
-    @pl.when(step == pl.num_programs(0) - 1)
-    def _():
-        contexts[...] = cacc[...].astype(F32)
-        words[...] = jnp.zeros_like(words)
-        for d in range(N_COL):
-            words[d, 0:4, :] = wacc[pl.ds(4 * d, 4), :]
-
-
-def count_sums(rows, cols, counts, group=16):
-    slots = counts.shape[0]
-    return pl.pallas_call(
-        functools.partial(count_kernel, group),
-        grid_spec=pltpu.PrefetchScalarGridSpec(
-            num_scalar_prefetch=2,
-            grid=(slots // group,),
-            in_specs=[pl.BlockSpec((group, T, T), lambda i, r, c: (i, 0, 0))],
-            out_specs=[
-                pl.BlockSpec((N_COL, 8, T), lambda i, r, c: (0, 0, 0)),
-                pl.BlockSpec((COL_TILES, T), lambda i, r, c: (0, 0)),
-            ],
-            scratch_shapes=[pltpu.VMEM((T, ROW_TILES), F32), pltpu.VMEM((COL_TILES, T), I32)],
-        ),
-        out_shape=[
-            jax.ShapeDtypeStruct((N_COL, 8, T), F32),
-            jax.ShapeDtypeStruct((COL_TILES, T), F32),
-        ],
-        name="count_sums",
-    )(rows, cols, counts)
+GROUP = 16
 
 
 def powers_of(totals):
@@ -104,8 +60,23 @@
     return root * jnp.sqrt(root)
 
 
-def totals_kernel(words, contexts, panel, words_all, contexts_all, band,
-                  wrecv, crecv, mine, wss, wrs, css, crs, ass, ars, pss, prs, lsem):
+def load_counts(counts, held, sem):
+    copies = []
+    for b in range(counts.shape[0] // GROUP):
+        part = pl.ds(b * GROUP, GROUP)
+        copies.append(pltpu.make_async_copy(counts.at[part], held.at[part], sem.at[b]))
+        copies[-1].start()
+    return copies
+
+
+def await_counts(counts, held, sem, b):
+    part = pl.ds(b * GROUP, GROUP)
+    pltpu.make_async_copy(counts.at[part], held.at[part], sem.at[b]).wait()
+
+
+def totals_kernel(rows, cols, counts, panel, words_all, contexts_all, band, held,
+                  wacc, words, contexts, wrecv, crecv, mine,
+                  cs, wss, wrs, css, crs, ass, ars, pss, prs, lsem):
     x, yl = lax.axis_index("x"), lax.axis_index("yl")
     z, yh, c = lax.axis_index("z"), lax.axis_index("yh"), lax.axis_index("core")
     row = yl * NX + x
@@ -124,16 +95,43 @@
                         ((dz * NYH + dy) * NC + dc, (pz * NYH + py) * NC + pc,
                          {"z": pz, "yh": py, "core": pc})
                     )
+    load_counts(counts, held, cs)
     greet([d for _, d in row_peers] + [d for _, _, d in col_peers])
-
-    waits = []
-    csends = [remote(contexts, crecv.at[k], css.at[k], crs.at[k], d) for k, d in row_peers]
-    wsends = [remote(words.at[p], wrecv.at[k], wss.at[k], wrs.at[k], d) for k, p, d in col_peers]
     psends = [remote(panel, band.at[row], pss.at[k], prs.at[k], d) for k, d in row_peers]
     own = pltpu.make_async_copy(panel, band.at[row], lsem.at[0])
-    for copy in csends + wsends + psends:
+    for copy in psends:
         copy.start()
     own.start()
+
+    wacc[...] = jnp.zeros_like(wacc)
+    lanes = lax.broadcasted_iota(I32, (T, T), 1)
+    bands = lax.broadcasted_iota(I32, (COL_TILES, T), 0)
+
+    def some(b, per_context):
+        await_counts(counts, held, cs, b)
+        per_word = wacc[...]
+        for g in range(GROUP):
+            slot = b * GROUP + g
+            value = held[slot]
+            per_context = per_context + jnp.where(
+                bands == cols[slot], jnp.sum(value, axis=0, keepdims=True), 0
+            )
+            sums = jnp.sum(value.astype(F32), axis=1, keepdims=True)
+            per_word = per_word + jnp.where(lanes == rows[slot], sums, 0.0)
+        wacc[...] = per_word
+        return per_context
+
+    per_context = lax.fori_loop(0, counts.shape[0] // GROUP, some, jnp.zeros((COL_TILES, T), I32))
+    contexts[...] = per_context.astype(F32)
+    csends = [remote(contexts, crecv.at[k], css.at[k], crs.at[k], d) for k, d in row_peers]
+    for copy in csends:
+        copy.start()
+    for d in range(N_COL):
+        words[d, 0:4, :] = wacc[pl.ds(4 * d, 4), :]
+        words[d, 4:8, :] = jnp.zeros((4, T), F32)
+    wsends = [remote(words.at[p], wrecv.at[k], wss.at[k], wrs.at[k], d) for k, p, d in col_peers]
+    for copy in wsends:
+        copy.start()
 
     for copy in csends:
         copy.wait_recv()
@@ -163,79 +161,77 @@
     own.wait()
 
 
-def totals(words, contexts, panel):
+def totals(rows, cols, counts, panel):
+    slots = counts.shape[0]
     return pl.pallas_call(
         totals_kernel,
-        in_specs=[VMEM, VMEM, ANY],
-        out_specs=[VMEM, VMEM, ANY],
+        in_specs=[SMEM, SMEM, ANY, ANY],
+        out_specs=[VMEM, VMEM, ANY, VMEM],
         out_shape=[
             jax.ShapeDtypeStruct((N_COL, 8, T), F32),
             jax.ShapeDtypeStruct((COL_TILES, T), F32),
             jax.ShapeDtypeStruct((N_ROW, SHARE, T), BF16),
+            jax.ShapeDtypeStruct((slots, T, T), I32),
         ],
         scratch_shapes=[
+            pltpu.VMEM((T, ROW_TILES), F32),
+            pltpu.VMEM((N_COL, 8, T), F32),
+            pltpu.VMEM((COL_TILES, T), F32),
             pltpu.VMEM((N_COL, 8, T), F32),
             pltpu.VMEM((N_ROW, COL_TILES, T), F32),
             pltpu.VMEM((8, T), F32),
+            DMA((slots // GROUP,)),
             DMA((N_COL,)), DMA((N_COL,)), DMA((N_ROW,)), DMA((N_ROW,)),
             DMA((N_COL,)), DMA((N_COL,)), DMA((N_ROW,)), DMA((N_ROW,)), DMA((1,)),
         ],
-        compiler_params=pltpu.CompilerParams(collective_id=0, has_side_effects=True),
+        compiler_params=pltpu.CompilerParams(collective_id=0, has_side_effects=True, vmem_limit_bytes=16 << 20),
         name="totals",
-    )(words, contexts, panel)
-
-
-def word_kernel(group, rows, cols, counts, words_all, contexts_all, band, tiles, partial,
+    )(rows, cols, counts, panel)
+
+
+def word_kernel(rows, cols, counts, words_all, contexts_all, band, tiles, partial,
                 word_term, context_log):
-    step = pl.program_id(0)
-
-    @pl.when(step == 0)
-    def _():
-        power = jnp.zeros((1, T), F32)
-        for d in range(N_COL):
-            word_term[pl.ds(4 * d, 4), :] = words_all[d, 0:4, :]
-            power = power + words_all[d, 4:5, :]
-        log_scale = jnp.log(power) - math.log(NEG_SAMPLES)
-        word_term[...] = log_scale - jnp.log(jnp.maximum(word_term[...], 1.0))
-        context_log[...] = jnp.log(jnp.maximum(powers_of(contexts_all[...]), 1.0))
-        partial[...] = jnp.zeros_like(partial)
-
-    lanes = lax.broadcasted_iota(I32, (T, T), 1)
-    for g in range(group):
-        slot = step * group + g
-        row, col = rows[slot], cols[slot]
-        value = counts[g]
-        per_word = jnp.sum(jnp.where(lanes == row, word_term[...], 0.0), axis=1, keepdims=True)
-        pointwise = jnp.log(value.astype(F32)) + per_word - context_log[pl.ds(col, 1), :]
-        tile = jnp.where(value > 0, jnp.maximum(pointwise, 0.0), 0.0).astype(BF16)
-        tiles[g] = tile
-        partial[row] += jnp.dot(tile, band[col], preferred_element_type=F32)
-
-
-def word_products(rows, cols, counts, words_all, contexts_all, band, group=16):
+    power = jnp.zeros((1, T), F32)
+    for d in range(N_COL):
+        word_term[pl.ds(4 * d, 4), :] = words_all[d, 0:4, :]
+        power = power + words_all[d, 4:5, :]
+    log_scale = jnp.log(power) - math.log(NEG_SAMPLES)
+    word_term[...] = log_scale - jnp.log(jnp.maximum(word_term[...], 1.0))
+    context_log[...] = jnp.log(jnp.maximum(powers_of(contexts_all[...]), 1.0))
+
+    def clear(t, carry):
+        partial[t] = jnp.zeros((T, T), F32)
+        return carry
+
+    lax.fori_loop(0, ROW_TILES, clear, 0, unroll=4)
+
+    def some(b, carry):
+        for g in range(GROUP):
+            slot = b * GROUP + g
+            row, col = rows[slot], cols[slot]
+            value = counts[slot]
+            per_word = jnp.take_along_axis(word_term[...], jnp.full((T, T), row, I32), axis=1)
+            pointwise = jnp.log(value.astype(F32)) + per_word - context_log[pl.ds(col, 1), :]
+            tile = jnp.where(value > 0, jnp.maximum(pointwise, 0.0), 0.0).astype(BF16)
+            tiles[slot] = tile
+            partial[row] += jnp.dot(tile, band[col], preferred_element_type=F32)
+        return carry
+
+    lax.fori_loop(0, counts.shape[0] // GROUP, some, 0)
+
+
+def word_products(rows, cols, counts, words_all, contexts_all, band):
     slots = counts.shape[0]
-    whole3 = lambda i, r, c: (0, 0, 0)
     return pl.pallas_call(
-        functools.partial(word_kernel, group),
-        grid_spec=pltpu.PrefetchScalarGridSpec(
-            num_scalar_prefetch=2,
-            grid=(slots // group,),
-            in_specs=[
-                pl.BlockSpec((group, T, T), lambda i, r, c: (i, 0, 0)),
-                pl.BlockSpec((N_COL, 8, T), whole3),
-                pl.BlockSpec((COL_TILES, T), lambda i, r, c: (0, 0)),
-                pl.BlockSpec((COL_TILES, T, T), whole3),
-            ],
-            out_specs=[
-                pl.BlockSpec((group, T, T), lambda i, r, c: (i, 0, 0)),
-                pl.BlockSpec((ROW_TILES, T, T), whole3),
-            ],
-            scratch_shapes=[pltpu.VMEM((T, ROW_TILES), F32), pltpu.VMEM((COL_TILES, T), F32)],
-        ),
+        word_kernel,
+        in_specs=[SMEM, SMEM, VMEM, VMEM, VMEM, VMEM],
+        out_specs=[VMEM, VMEM],
+        scratch_shapes=[pltpu.VMEM((T, ROW_TILES), F32), pltpu.VMEM((COL_TILES, T), F32)],
         out_shape=[
             jax.ShapeDtypeStruct((slots, T, T), BF16),
             jax.ShapeDtypeStruct((ROW_TILES, T, T), F32),
         ],
+        compiler_params=pltpu.CompilerParams(vmem_limit_bytes=28 << 20),
         name="word_products",
     )(rows, cols, counts, words_all, contexts_all, band)
 
@@ -253,18 +249,14 @@
 X_STEPS = chain_steps(NX // 2)
 
 
-def word_panel_kernel(partial, share, everyone, own, sib, sendb, recvb, ysend, yrecv, mine,
-                      lsem, xss, xrs, zss, zrs, yss, yrs, gss, grs, hss, hrs, ms):
+def word_panel_kernel(partial, share, everyone, sib, sendb, recvb, ysend, yrecv, mine,
+                      xss, xrs, zss, zrs, yss, yrs, gss, grs, hss, hrs, ms):
     z, yh, c = lax.axis_index("z"), lax.axis_index("yh"), lax.axis_index("core")
     ways = ({"z": lax.rem(z + 1, NZ)}, {"z": lax.rem(z + NZ - 1, NZ)})
     other_y, other_core = {"yh": 1 - yh}, {"core": 1 - c}
 
-    loads, swaps = {}, {}
+    swaps = {}
     order = [(dz, h) for dz in (4, 3, 5, 2, 6, 1, 7, 0) for h in range(2)]
-    for dz, h in order:
-        slot, zz = dz * 2 + h, lax.rem(z + dz, NZ)
-        loads[dz, h] = pltpu.make_async_copy(partial.at[zz, h, c], own.at[slot], lsem.at[slot])
-        loads[dz, h].start()
     greet([*ways, other_y, other_core])
     for dz, h in order:
         slot, zz = dz * 2 + h, lax.rem(z + dz, NZ)
@@ -272,9 +264,8 @@
         swaps[dz, h].start()
 
     def block(dz, h):
-        loads[dz, h].wait()
         swaps[dz, h].wait_recv()
-        return own[dz * 2 + h] + sib[dz * 2 + h]
+        return partial[lax.rem(z + dz, NZ), h, c] + sib[dz * 2 + h]
 
     sends = {}
     for n, (s, way, half) in enumerate(Z_STEPS):
@@ -290,13 +281,12 @@
 
     last = NZ // 2 - 1
     for h in range(2):
-        loads[0, h].wait()
         swaps[0, h].wait_recv()
         for way in range(2):
             sends[last, way, h][1].wait_recv()
 
     def arrived(h):
-        value = own[h] + sib[h]
+        value = partial[z, h, c] + sib[h]
         for way in range(2):
             first, second = sends[last, way, 0][0], sends[last, way, 1][0]
             value = value + decode(recvb.at[first + h * (second - first)])
@@ -371,58 +361,54 @@
     n = len(Z_STEPS)
     return pl.pallas_call(
         word_panel_kernel,
-        in_specs=[ANY],
+        in_specs=[VMEM],
         out_specs=[VMEM, ANY],
         out_shape=[
             jax.ShapeDtypeStruct((SHARE, T), F32),
             jax.ShapeDtypeStruct((NZ, NYH, NC, 4, T, T), BF16),
         ],
         scratch_shapes=[
-            pltpu.VMEM((2 * NZ, SHARE, T), F32),
             pltpu.VMEM((2 * NZ, SHARE, T), F32),
             pltpu.VMEM((n, CODE, T), I16),
             pltpu.VMEM((n, CODE, T), I16),
             pltpu.VMEM((CODE, T), I16),
             pltpu.VMEM((CODE, T), I16),
             pltpu.VMEM((4, T, T), BF16),
-            DMA((2 * NZ,)), DMA((2 * NZ,)), DMA((2 * NZ,)), DMA((n,)), DMA((n,)),
+            DMA((2 * NZ,)), DMA((2 * NZ,)), DMA((n,)), DMA((n,)),
             DMA((2,)), DMA((2,)), DMA((2 * NZ,)), DMA((2 * NZ,)),
             DMA((2 * NZ,)), DMA((2 * NZ,)), DMA((1,)),
         ],
-        compiler_params=pltpu.CompilerParams(collective_id=1, has_side_effects=True),
+        compiler_params=pltpu.CompilerParams(collective_id=1, has_side_effects=True, vmem_limit_bytes=16 << 20),
         name="word_panel_sum",
     )(partial)
 
 
-def context_kernel(group, rows, cols, tiles, rounded, partial):
-    step = pl.program_id(0)
-
-    @pl.when(step == 0)
-    def _():
-        partial[...] = jnp.zeros_like(partial)
-
-    for g in range(group):
-        slot = step * group + g
-        partial[cols[slot]] += jnp.dot(rounded[rows[slot]], tiles[g], preferred_element_type=F32)
-
-
-def context_products(rows, cols, tiles, rounded, group=16):
+def context_kernel(rows, cols, tiles, rounded, share, partial, share_out):
+    share_out[...] = share[...]
+    partial[...] = jnp.zeros_like(partial)
+
+    def some(b, carry):
+        for g in range(GROUP):
+            slot = b * GROUP + g
+            partial[cols[slot]] += jnp.dot(rounded[rows[slot]], tiles[slot], preferred_element_type=F32)
+        return carry
+
+    lax.fori_loop(0, tiles.shape[0] // GROUP, some, 0)
+
+
+def context_products(rows, cols, tiles, rounded, share):
     slots = tiles.shape[0]
-    whole3 = lambda i, r, c: (0, 0, 0)
     return pl.pallas_call(
-        functools.partial(context_kernel, group),
-        grid_spec=pltpu.PrefetchScalarGridSpec(
-            num_scalar_prefetch=2,
-            grid=(slots // group,),
-            in_specs=[
-                pl.BlockSpec((group, T, T), lambda i, r, c: (i, 0, 0)),
-                pl.BlockSpec((ROW_TILES, T, T), whole3),
-            ],
-            out_specs=pl.BlockSpec((COL_TILES, T, T), whole3),
-        ),
-        out_shape=jax.ShapeDtypeStruct((COL_TILES, T, T), F32),
+        context_kernel,
+        in_specs=[SMEM, SMEM, VMEM, VMEM, VMEM],
+        out_specs=[VMEM, VMEM],
+        out_shape=[
+            jax.ShapeDtypeStruct((COL_TILES, T, T), F32),
+            jax.ShapeDtypeStruct((SHARE, T), F32),
+        ],
+        compiler_params=pltpu.CompilerParams(vmem_limit_bytes=16 << 20),
         name="context_products",
-    )(rows, cols, tiles, rounded)
+    )(rows, cols, tiles, rounded, share)
 
 
 def context_panel_kernel(partial, share, sendb, recvb, ysend, yrecv, xss, xrs, yss, yrs):
@@ -480,20 +466,20 @@
             pltpu.VMEM((CODE, T), I16),
             DMA((n,)), DMA((n,)), DMA((1,)), DMA((1,)),
         ],
-        compiler_params=pltpu.CompilerParams(collective_id=2, has_side_effects=True),
+        compiler_params=pltpu.CompilerParams(collective_id=2, has_side_effects=True, vmem_limit_bytes=8 << 20),
         name="context_panel_sum",
     )(partial)
 
 
 def shards(tile_counts, tile_rows, tile_cols, panel):
     counts, rows, cols = tile_counts[0, 0], tile_rows[0, 0], tile_cols[0, 0]
-    words, contexts = count_sums(rows, cols, counts)
-    words_all, contexts_all, band = totals(words, contexts, panel)
+    counts = pltpu.with_memory_space_constraint(counts, pltpu.HBM)
+    words_all, contexts_all, band, held = totals(rows, cols, counts, panel)
     band = band.reshape(COL_TILES, T, T)
-    tiles, partial = word_products(rows, cols, counts, words_all, contexts_all, band)
+    tiles, partial = word_products(rows, cols, held, words_all, contexts_all, band)
     share, everyone = word_panel_sum(partial.reshape(NZ, NYH, NC, SHARE, T))
     rounded = everyone.reshape(ROW_TILES, T, T)
-    context_partial = context_products(rows, cols, tiles, rounded)
+    context_partial, share = context_products(rows, cols, tiles, rounded, share)
     context_share = context_panel_sum(context_partial.reshape(NYL, NX, SHARE, T))
     return share, context_share
 

time: 153 us -> 129 us (0.84)
  Pallas kernels: 149 us -> 124 us
    pallas_call x5 -> x4, Pallas kernels: 128 us -> 107 us  [the longest x1 61.2 us: word_panel_sum(): pl.pallas_call(word_panel_kernel, in_specs=[VMEM], out_specs=[VMEM, ANY],...]
    pallas_call x1, Pallas kernels: 21 us -> 17.2 us  [context_panel_sum(): pl.pallas_call(context_panel_kernel, in_specs=[VMEM], out_specs=VMEM, out...]
where the time goes in v2:
time: 129 us; the launch traced here: 128 us
  Pallas kernels  124 us (96%)
  local copies, waits for them, and re-layouts  2.98 us (2%)
    pallas_call x1, Pallas kernels, word_panel_sum(): pl.pallas_call(word_panel_kernel, in_specs=[VMEM], out_specs=[VMEM, ANY],...  61.2 us
    pallas_call x1, Pallas kernels, totals(): pl.pallas_call(totals_kernel, in_specs=[SMEM, SMEM, ANY, ANY], out_specs=...  34.4 us
    pallas_call x1, Pallas kernels, context_panel_sum(): pl.pallas_call(context_panel_kernel, in_specs=[VMEM], out_specs=VMEM, out...  17.2 us
    pallas_call x1, Pallas kernels, word_products(): pl.pallas_call(word_kernel, in_specs=[SMEM, SMEM, VMEM, VMEM, VMEM, VMEM]...  7.07 us
    pallas_call x1, Pallas kernels, context_products(): pl.pallas_call(context_kernel, in_specs=[SMEM, SMEM, VMEM, VMEM, VMEM], o...  4.42 us
    unnamed x11, local copies, waits for them, and re-layouts  2.98 us

profile of v2, /device:TPU:8, one launch (start us, length us, event | category | flops | bytes accessed | tf_op | source)
XLA Modules:
  0.0 127.9 jit_solution(14627453638737606551)
XLA Ops:
  0.6 0.0 copy-start.4
  0.6 0.0 copy-start.2
  0.7 0.0 copy-start
  0.7 0.9 copy-done
  1.6 0.0 copy-start.1
  1.6 0.7 copy-done.1
  2.2 0.0 copy-start.3
  2.2 0.7 copy-done.3
  2.9 34.4 %totals.1 = (f32[32,8,128]{2,1,0:T(8,128)S(1)}, f32[32,128]{1,0:T(8,128)S(1)}, bf16[8,512,128]{2,1,0:T(8,128)(2,1)S(1)}, s32[160,128,128]{2,1,0:T(8,128)S(1)}) custom-call(s32[160]{0:T(256)S(1)} %bitcast.11, s32[160]{0:T(256)S(1)} %bitcast.14, s32[160,128,128]{2,1,0:T(8,128)} %bitcast.17, bf16[512,128]{1,0:T(8,128)(2,1)S(1)} %copy-done), custom_call_target="tpu_custom_call" | custom-call | tf_op jit(solution)/shard_map/totals/pallas_call | solution.py:166
  37.3 0.0 copy-done.4
  37.3 0.0 copy-done.2
  37.3 7.1 %word_products.1 = (bf16[160,128,128]{2,1,0:T(8,128)(2,1)S(1)}, f32[128,128,128]{2,1,0:T(8,128)S(1)}) custom-call(s32[160]{0:T(256)S(1)} %bitcast.12, s32[160]{0:T(256)S(1)} %bitcast.15, s32[160,128,128]{2,1,0:T(8,128)S(1)} %get-tuple-element.12.counts, f32[32,8,128]{2,1,0:T(8,128)S(1)} %get-tuple-element.13.words_all, ...), custom_call_target="tpu_custom_call" | custom-call | tf_op jit(solution)/shard_map/word_products/pallas_call | solution.py:225
  44.4 61.2 %word_panel_sum.1 = (f32[512,128]{1,0:T(8,128)S(1)}, bf16[8,2,2,4,128,128]{5,4,3,2,1,0:T(8,128)(2,1)S(1)}) custom-call(f32[8,2,2,512,128]{4,3,2,1,0:T(8,128)S(1)} %bitcast.7), custom_call_target="tpu_custom_call" | custom-call | tf_op jit(solution)/shard_map/word_panel_sum/pallas_call | solution.py:362
  105.6 4.4 %context_products.1 = (f32[32,128,128]{2,1,0:T(8,128)S(1)}, f32[512,128]{1,0:T(8,128)}) custom-call(s32[160]{0:T(256)S(1)} %bitcast.13, s32[160]{0:T(256)S(1)} %bitcast.16, bf16[160,128,128]{2,1,0:T(8,128)(2,1)S(1)} %get-tuple-element.16.tiles, bf16[128,128,128]{2,1,0:T(8,128)(2,1)S(1)} %bitcast.8, f32[512,128]{1,0:T(8,128)S(1)} %get-tuple-element.19.share), custom_call_target="tpu_custom_call" | custom-call | tf_op jit(solution)/shard_map/context_products/pallas_call | solution.py:401
  110.1 17.2 %context_panel_sum.1 = f32[512,128]{1,0:T(8,128)S(1)} custom-call(f32[2,4,512,128]{3,2,1,0:T(8,128)S(1)} %bitcast.9), custom_call_target="tpu_custom_call" | custom-call | tf_op jit(solution)/shard_map/context_panel_sum/pallas_call | solution.py:457
  127.2 0.7 copy.7
Async XLA Ops:
  0.6 36.7 %copy-start.4 = (s32[1,1,160]{2,1,0:T(1,128)S(1)}, s32[1,1,160]{2,1,0:T(1,128)}, u32[]{:S(2)}) copy-start(s32[1,1,160]{2,1,0:T(1,128)} %param.6) | copy-start | bytes 1924
  0.6 36.7 %copy-start.2 = (s32[1,1,160]{2,1,0:T(1,128)S(1)}, s32[1,1,160]{2,1,0:T(1,128)}, u32[]{:S(2)}) copy-start(s32[1,1,160]{2,1,0:T(1,128)} %param.5) | copy-start | bytes 1924
  0.7 0.9 copy-start
  1.6 0.7 copy-start.1
  2.2 0.7 copy-start.3

commit v3 on v2

--- a/solution.py
+++ b/solution.py
@@ -15,7 +15,8 @@
 N_ROW, N_COL = NX * NYL, NZ * NYH * NC
 ROW_TILES, COL_TILES = 128, 32
 SHARE = 512
-CODE = SHARE + 16
+HALF = SHARE // 2
+CODE = HALF + 16
 MESH = pl.DeviceIdType.MESH
 F32, BF16, I32, I16 = jnp.float32, jnp.bfloat16, jnp.int32, jnp.int16
 ANY = pl.BlockSpec(memory_space=pl.ANY)
@@ -43,13 +44,13 @@
     top = jnp.max(jnp.abs(value), axis=0, keepdims=True)
     expo = jnp.ceil(jnp.log(jnp.maximum(top, 1e-30)) * (1.0 / LN2) + 0.001) - 14.0
     scaled = jnp.round(value * jnp.exp(expo * -LN2))
-    ref[pl.ds(0, SHARE), :] = scaled.astype(I32).astype(I16)
-    ref[pl.ds(SHARE, 16), :] = jnp.broadcast_to(expo, (16, T)).astype(I32).astype(I16)
+    ref[pl.ds(0, HALF), :] = scaled.astype(I32).astype(I16)
+    ref[pl.ds(HALF, 16), :] = jnp.broadcast_to(expo, (16, T)).astype(I32).astype(I16)
 
 
 def decode(ref):
-    expo = ref[pl.ds(SHARE, 16), :].astype(I32).astype(F32)[0:1]
-    return ref[pl.ds(0, SHARE), :].astype(I32).astype(F32) * jnp.exp(expo * LN2)
+    expo = ref[pl.ds(HALF, 16), :].astype(I32).astype(F32)[0:1]
+    return ref[pl.ds(0, HALF), :].astype(I32).astype(F32) * jnp.exp(expo * LN2)
 
 
 GROUP = 16
@@ -97,10 +98,10 @@
                     )
     load_counts(counts, held, cs)
     greet([d for _, d in row_peers] + [d for _, _, d in col_peers])
-    psends = [remote(panel, band.at[row], pss.at[k], prs.at[k], d) for k, d in row_peers]
+    psends = {k: remote(panel, band.at[row], pss.at[k], prs.at[k], d) for k, d in row_peers}
     own = pltpu.make_async_copy(panel, band.at[row], lsem.at[0])
-    for copy in psends:
-        copy.start()
+    for dx, dy in ((1, 0), (3, 0), (0, 1)):
+        psends[dx * NYL + dy].start()
     own.start()
 
     wacc[...] = jnp.zeros_like(wacc)
@@ -132,6 +133,8 @@
     wsends = [remote(words.at[p], wrecv.at[k], wss.at[k], wrs.at[k], d) for k, p, d in col_peers]
     for copy in wsends:
         copy.start()
+    for dx, dy in ((1, 1), (3, 1)):
+        psends[dx * NYL + dy].start()
 
     for copy in csends:
         copy.wait_recv()
@@ -151,12 +154,14 @@
     asends = [remote(mine, words_all.at[col], ass.at[k], ars.at[k], d) for k, _, d in col_peers]
     for copy in asends:
         copy.start()
+    for dx, dy in ((2, 0), (2, 1)):
+        psends[dx * NYL + dy].start()
     words_all[col] = mine[...]
     for copy in asends:
         copy.wait()
     for copy in csends + wsends:
         copy.wait_send()
-    for copy in psends:
+    for copy in psends.values():
         copy.wait()
     own.wait()
 
@@ -236,129 +241,205 @@
     )(rows, cols, counts, words_all, contexts_all, band)
 
 
-def chain_steps(length):
+AWAY = (0, 1, 0)
+
+
+def lane_steps(length):
     steps = []
     for s in range(length):
-        for way, half in ((0, 1), (1, 0), (0, 0), (1, 1)):
-            if s > 0 or way == half:
-                steps.append((s, way, half))
+        for lanes in ((0, 1), (2,)):
+            for far in (False, True):
+                for lane in lanes:
+                    for way in range(2):
+                        if (way == AWAY[lane]) == far and (far or s):
+                            steps.append((s, way, lane))
     return steps
 
 
-Z_STEPS = chain_steps(NZ // 2)
-X_STEPS = chain_steps(NX // 2)
-
-
-def word_panel_kernel(partial, share, everyone, sib, sendb, recvb, ysend, yrecv, mine,
-                      xss, xrs, zss, zrs, yss, yrs, gss, grs, hss, hrs, ms):
-    z, yh, c = lax.axis_index("z"), lax.axis_index("yh"), lax.axis_index("core")
-    ways = ({"z": lax.rem(z + 1, NZ)}, {"z": lax.rem(z + NZ - 1, NZ)})
-    other_y, other_core = {"yh": 1 - yh}, {"core": 1 - c}
-
-    swaps = {}
-    order = [(dz, h) for dz in (4, 3, 5, 2, 6, 1, 7, 0) for h in range(2)]
-    greet([*ways, other_y, other_core])
-    for dz, h in order:
-        slot, zz = dz * 2 + h, lax.rem(z + dz, NZ)
-        swaps[dz, h] = remote(partial.at[zz, h, 1 - c], sib.at[slot], xss.at[slot], xrs.at[slot], other_core)
-        swaps[dz, h].start()
-
-    def block(dz, h):
-        swaps[dz, h].wait_recv()
-        return partial[lax.rem(z + dz, NZ), h, c] + sib[dz * 2 + h]
-
-    sends = {}
-    for n, (s, way, half) in enumerate(Z_STEPS):
-        value = block((NZ // 2 - s) if way == 0 else (NZ // 2 + s), half)
-        if (s - 1, way, half) in sends:
-            before = sends[s - 1, way, half]
-            before[1].wait_recv()
-            value = value + decode(recvb.at[before[0]])
+Z_STEPS = lane_steps(NZ // 2)
+X_STEPS = lane_steps(NX // 2)
+
+
+def ring_sum(steps, length, y, raw, ready, ways, other_y, sendb, recvb, ysendb, yrecvb,
+             ss, rs, yss, yrs):
+    trades, sends, traded = {}, {}, set()
+
+    def trade(d):
+        ready(d)
+        encode(raw(d, 1 - y, 1), ysendb.at[d])
+        trades[d] = remote(ysendb.at[d], yrecvb.at[d], yss.at[d], yrs.at[d], other_y)
+        trades[d].start()
+
+    def term(d, lane):
+        if lane < 2:
+            return raw(d, lane, 0)
+        if d not in traded:
+            trades[d].wait_recv()
+            traded.add(d)
+        return raw(d, y, 1) + decode(yrecvb.at[d])
+
+    trade(length)
+    for n, (s, way, lane) in enumerate(steps):
+        if lane == 2 and (n == 0 or steps[n - 1][2] != 2):
+            for d in sorted({length - s - 1, (length + s + 1) % (2 * length)}):
+                trade(d)
+        d = length - s if way == 0 else length + s
+        value = term(d, lane)
+        if (s - 1, way, lane) in sends:
+            index, before = sends[s - 1, way, lane]
+            before.wait_recv()
+            value = value + decode(recvb.at[index])
         encode(value, sendb.at[n])
-        copy = remote(sendb.at[n], recvb.at[n], zss.at[n], zrs.at[n], ways[way])
+        copy = remote(sendb.at[n], recvb.at[n], ss.at[n], rs.at[n], ways[way])
         copy.start()
-        sends[s, way, half] = (n, copy)
-
-    last = NZ // 2 - 1
-    for h in range(2):
-        swaps[0, h].wait_recv()
+        sends[s, way, lane] = (n, copy)
+
+    last = length - 1
+    for lane in (0, 1):
         for way in range(2):
-            sends[last, way, h][1].wait_recv()
+            sends[last, way, lane][1].wait_recv()
 
     def arrived(h):
-        value = partial[z, h, c] + sib[h]
+        value = raw(0, h, 0)
         for way in range(2):
             first, second = sends[last, way, 0][0], sends[last, way, 1][0]
             value = value + decode(recvb.at[first + h * (second - first)])
         return value
 
-    encode(arrived(1 - yh), ysend)
-    ycopy = remote(ysend, yrecv, yss.at[0], yrs.at[0], other_y)
-    ycopy.start()
-    kept = arrived(yh)
-    ycopy.wait_recv()
-    total = kept + decode(yrecv)
-    share[...] = total
-    for t in range(4):
-        mine[t] = total[t * T : (t + 1) * T].T.astype(BF16)
-
-    halves = (yh, 1 - yh)
-    home = everyone.at[z, yh, c]
-    keep = pltpu.make_async_copy(mine, home, ms.at[0])
+    end = 2 * length
+    encode(arrived(1 - y), ysendb.at[end])
+    swap = remote(ysendb.at[end], yrecvb.at[end], yss.at[end], yrs.at[end], other_y)
+    swap.start()
+    second = term(0, 2)
+    for way in range(2):
+        index, copy = sends[last, way, 2]
+        copy.wait_recv()
+        second = second + decode(recvb.at[index])
+    first = arrived(y)
+    swap.wait_recv()
+    first = first + decode(yrecvb.at[end])
+
+    def drain():
+        for _, copy in sends.values():
+            copy.wait_send()
+        for copy in trades.values():
+            copy.wait_send()
+        swap.wait_send()
+
+    return first, second, drain
+
+
+def ring_scratch(steps, length):
+    n, y = len(steps), 2 * length + 1
+    return [
+        pltpu.VMEM((n, CODE, T), I16), pltpu.VMEM((n, CODE, T), I16),
+        pltpu.VMEM((y, CODE, T), I16), pltpu.VMEM((y, CODE, T), I16),
+        DMA((n,)), DMA((n,)), DMA((y,)), DMA((y,)),
+    ]
+
+
+def word_panel_kernel(partial, share, everyone, sib, mine, xss, xrs, gss, grs, hss, hrs, pss, prs, ms,
+                      *ring):
+    z, yh, c = lax.axis_index("z"), lax.axis_index("yh"), lax.axis_index("core")
+    ways = ({"z": lax.rem(z + 1, NZ)}, {"z": lax.rem(z + NZ - 1, NZ)})
+    other_y, other_core = {"yh": 1 - yh}, {"core": 1 - c}
+    length = NZ // 2
+
+    greet([*ways, other_y, other_core])
+    swaps = {}
+    for dz in (4, 3, 5, 2, 6, 1, 7, 0):
+        for h in range(2):
+            slot, zz = dz * 2 + h, lax.rem(z + dz, NZ)
+            swaps[dz, h] = remote(partial.at[zz, h, 1 - c], sib.at[slot], xss.at[slot], xrs.at[slot], other_core)
+            swaps[dz, h].start()
+
+    def ready(d):
+        for h in range(2):
+            swaps[d, h].wait_recv()
+
+    def raw(d, h, part):
+        rows = pl.ds(part * HALF, HALF)
+        return partial[lax.rem(z + d, NZ), h, c, rows, :] + sib[d * 2 + h, rows, :]
+
+    first, second, drain = ring_sum(Z_STEPS, length, yh, raw, ready, ways, other_y, *ring)
+    for part, total in enumerate((first, second)):
+        share[pl.ds(part * HALF, HALF), :] = total
+        for t in range(2):
+            mine[part * 2 + t] = total[t * T : (t + 1) * T].T.astype(BF16)
+
+    pair = (pl.ds(0, 2), pl.ds(2, 2))
+
+    def place(d, h, part):
+        return everyone.at[lax.rem(z + d, NZ), h, c, pair[part]]
+
+    keep = pltpu.make_async_copy(mine, everyone.at[z, yh, c], ms.at[0])
     keep.start()
-    ygive = remote(mine, home, yss.at[1], yrs.at[1], other_y)
-    ygive.start()
-    gives, hands = {}, []
-
-    def hand(src, place, k):
-        copy = remote(src, place, hss.at[k], hrs.at[k], other_core)
+    gives, hands, passes = {}, [], {}
+
+    def hand(src, dst, k):
+        copy = remote(src, dst, hss.at[k], hrs.at[k], other_core)
         copy.start()
         hands.append(copy)
 
-    def give(s, way, r, src):
-        zz = lax.rem(z + (NZ - s if way == 0 else s), NZ)
-        place = everyone.at[zz, halves[r], c]
-        k = (s * 2 + way) * 2 + r
-        copy = remote(place if src is None else src, place, gss.at[k], grs.at[k], ways[way])
-        copy.start()
-        gives[s, way, r] = copy
-
-    give(0, 0, 0, mine)
-    give(0, 1, 0, mine)
-    hand(mine, home, 0)
-    ygive.wait_recv()
-    give(0, 0, 1, None)
-    give(0, 1, 1, None)
-    hand(everyone.at[z, 1 - yh, c], everyone.at[z, 1 - yh, c], 1)
-    k = 2
-    for s in range(1, NZ // 2 + 1):
-        for r in range(2):
+    def along_y(src, dst, k):
+        passes[k] = remote(src, dst, pss.at[k], prs.at[k], other_y)
+        passes[k].start()
+
+    def lane_place(d, lane):
+        return place(d, 1 - yh if lane == 1 else yh, 1 if lane == 2 else 0)
+
+    def give(s, way, lane, src=None):
+        dst = lane_place((NZ - s) % NZ if way == 0 else s, lane)
+        k = (s * 2 + way) * 3 + lane
+        gives[s, way, lane] = remote(dst if src is None else src, dst, gss.at[k], grs.at[k], ways[way])
+        gives[s, way, lane].start()
+
+    own = (mine.at[pair[0]], mine.at[pair[1]])
+    along_y(own[0], place(0, yh, 0), NZ)
+    for way in range(2):
+        give(0, way, 2, own[1])
+    for way in range(2):
+        give(0, way, 0, own[0])
+    along_y(own[1], place(0, yh, 1), 0)
+    hand(own[0], place(0, yh, 0), 0)
+    hand(own[1], place(0, yh, 1), 2 * NZ)
+    passes[NZ].wait_recv()
+    for way in range(2):
+        give(0, way, 1)
+    hand(lane_place(0, 1), lane_place(0, 1), 1)
+    due = [0]
+    for s in range(1, length + 1):
+        came = []
+        for lane in (2, 0, 1):
             for way in range(2):
-                if (s - 1, way, r) not in gives:
+                if (s - 1, way, lane) not in gives:
                     continue
-                gives[s - 1, way, r].wait_recv()
-                if s < last or (s == last and way == r):
-                    give(s, way, r, None)
-                zz = lax.rem(z + (NZ - s if way == 0 else s), NZ)
-                place = everyone.at[zz, halves[r], c]
-                hand(place, place, k)
-                k += 1
+                gives[s - 1, way, lane].wait_recv()
+                if s < length - 1 or (s == length - 1 and way == AWAY[lane]):
+                    give(s, way, lane)
+                d = (NZ - s) % NZ if way == 0 else s
+                at = lane_place(d, lane)
+                if lane == 2:
+                    along_y(at, at, d)
+                    came.append(d)
+                hand(at, at, 2 * NZ + d if lane == 2 else d * 2 + lane)
+        for d in due:
+            passes[d].wait_recv()
+            hand(place(d, 1 - yh, 1), place(d, 1 - yh, 1), 3 * NZ + d)
+        due = came
+    for d in due:
+        passes[d].wait_recv()
+        hand(place(d, 1 - yh, 1), place(d, 1 - yh, 1), 3 * NZ + d)
 
     for copy in hands:
         copy.wait()
-    for copy in gives.values():
+    for copy in list(gives.values()) + list(passes.values()) + list(swaps.values()):
         copy.wait_send()
-    for _, copy in sends.values():
-        copy.wait_send()
-    for copy in swaps.values():
-        copy.wait_send()
-    ycopy.wait_send()
-    ygive.wait_send()
+    drain()
     keep.wait()
 
 
 def word_panel_sum(partial):
-    n = len(Z_STEPS)
     return pl.pallas_call(
         word_panel_kernel,
         in_specs=[VMEM],
@@ -369,14 +450,10 @@
         ],
         scratch_shapes=[
             pltpu.VMEM((2 * NZ, SHARE, T), F32),
-            pltpu.VMEM((n, CODE, T), I16),
-            pltpu.VMEM((n, CODE, T), I16),
-            pltpu.VMEM((CODE, T), I16),
-            pltpu.VMEM((CODE, T), I16),
             pltpu.VMEM((4, T, T), BF16),
-            DMA((2 * NZ,)), DMA((2 * NZ,)), DMA((n,)), DMA((n,)),
-            DMA((2,)), DMA((2,)), DMA((2 * NZ,)), DMA((2 * NZ,)),
-            DMA((2 * NZ,)), DMA((2 * NZ,)), DMA((1,)),
+            DMA((2 * NZ,)), DMA((2 * NZ,)), DMA((3 * NZ,)), DMA((3 * NZ,)),
+            DMA((4 * NZ,)), DMA((4 * NZ,)), DMA((NZ + 1,)), DMA((NZ + 1,)), DMA((1,)),
+            *ring_scratch(Z_STEPS, NZ // 2),
         ],
         compiler_params=pltpu.CompilerParams(collective_id=1, has_side_effects=True, vmem_limit_bytes=16 << 20),
         name="word_panel_sum",
@@ -411,61 +488,32 @@
     )(rows, cols, tiles, rounded, share)
 
 
-def context_panel_kernel(partial, share, sendb, recvb, ysend, yrecv, xss, xrs, yss, yrs):
+def context_panel_kernel(partial, share, *ring):
     x, yl = lax.axis_index("x"), lax.axis_index("yl")
     ways = ({"x": lax.rem(x + 1, NX)}, {"x": lax.rem(x + NX - 1, NX)})
     other_y = {"yl": 1 - yl}
     greet([*ways, other_y])
-    sends = {}
-    for n, (s, way, half) in enumerate(X_STEPS):
-        value = partial[half, lax.rem(x + (NX // 2 - s if way == 0 else NX // 2 + s), NX)]
-        if (s - 1, way, half) in sends:
-            before = sends[s - 1, way, half]
-            before[1].wait_recv()
-            value = value + decode(recvb.at[before[0]])
-        encode(value, sendb.at[n])
-        copy = remote(sendb.at[n], recvb.at[n], xss.at[n], xrs.at[n], ways[way])
-        copy.start()
-        sends[s, way, half] = (n, copy)
-    last = NX // 2 - 1
-    for h in range(2):
-        for way in range(2):
-            sends[last, way, h][1].wait_recv()
-
-    def arrived(h):
-        value = partial[h, x]
-        for way in range(2):
-            first, second = sends[last, way, 0][0], sends[last, way, 1][0]
-            value = value + decode(recvb.at[first + h * (second - first)])
-        return value
-
-    encode(arrived(1 - yl), ysend)
-    ycopy = remote(ysend, yrecv, yss.at[0], yrs.at[0], other_y)
-    ycopy.start()
-    kept = arrived(yl)
-    ycopy.wait_recv()
-    total = (kept + decode(yrecv)) * (1.0 / T)
-    for t in range(4):
-        share[pl.ds(t * T, T), :] = total[t * T : (t + 1) * T].T
-    for _, copy in sends.values():
-        copy.wait_send()
-    ycopy.wait_send()
+
+    def raw(d, h, part):
+        return partial[h, lax.rem(x + d, NX), pl.ds(part * HALF, HALF), :]
+
+    first, second, drain = ring_sum(
+        X_STEPS, NX // 2, yl, raw, lambda d: None, ways, other_y, *ring
+    )
+    for part, total in enumerate((first, second)):
+        total = total * (1.0 / T)
+        for t in range(2):
+            share[pl.ds(part * HALF + t * T, T), :] = total[t * T : (t + 1) * T].T
+    drain()
 
 
 def context_panel_sum(partial):
-    n = len(X_STEPS)
     return pl.pallas_call(
         context_panel_kernel,
         in_specs=[VMEM],
         out_specs=VMEM,
         out_shape=jax.ShapeDtypeStruct((SHARE, T), F32),
-        scratch_shapes=[
-            pltpu.VMEM((n, CODE, T), I16),
-            pltpu.VMEM((n, CODE, T), I16),
-            pltpu.VMEM((CODE, T), I16),
-            pltpu.VMEM((CODE, T), I16),
-            DMA((n,)), DMA((n,)), DMA((1,)), DMA((1,)),
-        ],
+        scratch_shapes=ring_scratch(X_STEPS, NX // 2),
         compiler_params=pltpu.CompilerParams(collective_id=2, has_side_effects=True, vmem_limit_bytes=8 << 20),
         name="context_panel_sum",
     )(partial)

time: 129 us -> 122 us (0.946)
  Pallas kernels: 124 us -> 117 us
    pallas_call x1, Pallas kernels: 61.2 us -> 53.2 us  [word_panel_sum(): pl.pallas_call(word_panel_kernel, in_specs=[VMEM], out_specs=[VMEM, ANY],...]
where the time goes in v3:
time: 122 us; the launch traced here: 121 us
  Pallas kernels  117 us (96%)
  local copies, waits for them, and re-layouts  2.98 us (2%)
    pallas_call x1, Pallas kernels, word_panel_sum(): pl.pallas_call(word_panel_kernel, in_specs=[VMEM], out_specs=[VMEM, ANY],...  53.2 us
    pallas_call x1, Pallas kernels, totals(): pl.pallas_call(totals_kernel, in_specs=[SMEM, SMEM, ANY, ANY], out_specs=...  35.5 us
    pallas_call x1, Pallas kernels, context_panel_sum(): pl.pallas_call(context_panel_kernel, in_specs=[VMEM], out_specs=VMEM, out...  16.8 us
    pallas_call x1, Pallas kernels, word_products(): pl.pallas_call(word_kernel, in_specs=[SMEM, SMEM, VMEM, VMEM, VMEM, VMEM]...  7.07 us
    pallas_call x1, Pallas kernels, context_products(): pl.pallas_call(context_kernel, in_specs=[SMEM, SMEM, VMEM, VMEM, VMEM], o...  4.42 us
    unnamed x11, local copies, waits for them, and re-layouts  2.98 us

profile of v3, /device:TPU:8, one launch (start us, length us, event | category | flops | bytes accessed | tf_op | source)
XLA Modules:
  0.0 120.7 jit_solution(6593102023114298725)
XLA Ops:
  0.6 0.0 copy-start.4
  0.6 0.0 copy-start.2
  0.7 0.0 copy-start
  0.7 0.9 copy-done
  1.6 0.0 copy-start.1
  1.6 0.7 copy-done.1
  2.2 0.0 copy-start.3
  2.2 0.7 copy-done.3
  2.9 35.5 %totals.1 = (f32[32,8,128]{2,1,0:T(8,128)S(1)}, f32[32,128]{1,0:T(8,128)S(1)}, bf16[8,512,128]{2,1,0:T(8,128)(2,1)S(1)}, s32[160,128,128]{2,1,0:T(8,128)S(1)}) custom-call(s32[160]{0:T(256)S(1)} %bitcast.11, s32[160]{0:T(256)S(1)} %bitcast.14, s32[160,128,128]{2,1,0:T(8,128)} %bitcast.17, bf16[512,128]{1,0:T(8,128)(2,1)S(1)} %copy-done), custom_call_target="tpu_custom_call" | custom-call | tf_op jit(solution)/shard_map/totals/pallas_call | solution.py:171
  38.4 0.0 copy-done.4
  38.4 0.0 copy-done.2
  38.5 7.1 %word_products.1 = (bf16[160,128,128]{2,1,0:T(8,128)(2,1)S(1)}, f32[128,128,128]{2,1,0:T(8,128)S(1)}) custom-call(s32[160]{0:T(256)S(1)} %bitcast.12, s32[160]{0:T(256)S(1)} %bitcast.15, s32[160,128,128]{2,1,0:T(8,128)S(1)} %get-tuple-element.12.counts, f32[32,8,128]{2,1,0:T(8,128)S(1)} %get-tuple-element.13.words_all, ...), custom_call_target="tpu_custom_call" | custom-call | tf_op jit(solution)/shard_map/word_products/pallas_call | solution.py:230
  45.5 53.2 %word_panel_sum.1 = (f32[512,128]{1,0:T(8,128)S(1)}, bf16[8,2,2,4,128,128]{5,4,3,2,1,0:T(8,128)(2,1)S(1)}) custom-call(f32[8,2,2,512,128]{4,3,2,1,0:T(8,128)S(1)} %bitcast.7), custom_call_target="tpu_custom_call" | custom-call | tf_op jit(solution)/shard_map/word_panel_sum/pallas_call | solution.py:443
  98.7 4.4 %context_products.1 = (f32[32,128,128]{2,1,0:T(8,128)S(1)}, f32[512,128]{1,0:T(8,128)}) custom-call(s32[160]{0:T(256)S(1)} %bitcast.13, s32[160]{0:T(256)S(1)} %bitcast.16, bf16[160,128,128]{2,1,0:T(8,128)(2,1)S(1)} %get-tuple-element.16.tiles, bf16[128,128,128]{2,1,0:T(8,128)(2,1)S(1)} %bitcast.8, f32[512,128]{1,0:T(8,128)S(1)} %get-tuple-element.19.share), custom_call_target="tpu_custom_call" | custom-call | tf_op jit(solution)/shard_map/context_products/pallas_call | solution.py:478
  103.1 16.8 %context_panel_sum.1 = f32[512,128]{1,0:T(8,128)S(1)} custom-call(f32[2,4,512,128]{3,2,1,0:T(8,128)S(1)} %bitcast.9), custom_call_target="tpu_custom_call" | custom-call | tf_op jit(solution)/shard_map/context_panel_sum/pallas_call | solution.py:511
  120.0 0.7 copy.7
Async XLA Ops:
  0.6 37.8 %copy-start.4 = (s32[1,1,160]{2,1,0:T(1,128)S(1)}, s32[1,1,160]{2,1,0:T(1,128)}, u32[]{:S(2)}) copy-start(s32[1,1,160]{2,1,0:T(1,128)} %param.6) | copy-start | bytes 1924
  0.6 37.8 %copy-start.2 = (s32[1,1,160]{2,1,0:T(1,128)S(1)}, s32[1,1,160]{2,1,0:T(1,128)}, u32[]{:S(2)}) copy-start(s32[1,1,160]{2,1,0:T(1,128)} %param.5) | copy-start | bytes 1924
  0.7 0.9 copy-start
  1.6 0.7 copy-start.1
  2.2 0.7 copy-start.3

commit v4 on v3

--- a/solution.py
+++ b/solution.py
@@ -33,11 +33,20 @@
     )
 
 
+def hail(devices):
+    for device in devices:
+        pl.semaphore_signal(
+            pltpu.get_barrier_semaphore(), inc=1, device_id=device, device_id_type=MESH
+        )
+
+
+def await_hails(devices):
+    pl.semaphore_wait(pltpu.get_barrier_semaphore(), len(devices))
+
+
 def greet(devices):
-    barrier = pltpu.get_barrier_semaphore()
-    for device in devices:
-        pl.semaphore_signal(barrier, inc=1, device_id=device, device_id_type=MESH)
-    pl.semaphore_wait(barrier, len(devices))
+    hail(devices)
+    await_hails(devices)
 
 
 def encode(value, ref):
@@ -75,13 +84,15 @@
     pltpu.make_async_copy(counts.at[part], held.at[part], sem.at[b]).wait()
 
 
-def totals_kernel(rows, cols, counts, panel, words_all, contexts_all, band, held,
-                  wacc, words, contexts, wrecv, crecv, mine,
+def totals_kernel(rows_in, cols_in, counts, panel, words_all, band, base,
+                  held, rows, cols, wacc, words, contexts, context_log, wrecv, crecv, mine,
                   cs, wss, wrs, css, crs, ass, ars, pss, prs, lsem):
     x, yl = lax.axis_index("x"), lax.axis_index("yl")
     z, yh, c = lax.axis_index("z"), lax.axis_index("yh"), lax.axis_index("core")
+    blocks = counts.shape[0] // GROUP
     row = yl * NX + x
     col = (z * NYH + yh) * NC + c
+    right, left = lax.rem(x + 1, NX), lax.rem(x + NX - 1, NX)
     row_peers = [
         (dx * NYL + dy, {"x": lax.rem(x + dx, NX), "yl": lax.rem(yl + dy, NYL)})
         for dx in range(NX) for dy in range(NYL) if dx or dy
@@ -96,17 +107,23 @@
                         ((dz * NYH + dy) * NC + dc, (pz * NYH + py) * NC + pc,
                          {"z": pz, "yh": py, "core": pc})
                     )
+    everybody = [d for _, d in row_peers] + [d for _, _, d in col_peers]
+    hail(everybody)
+    slots = [
+        pltpu.make_async_copy(rows_in, rows, lsem.at[1]),
+        pltpu.make_async_copy(cols_in, cols, lsem.at[2]),
+    ]
+    for copy in slots:
+        copy.start()
     load_counts(counts, held, cs)
-    greet([d for _, d in row_peers] + [d for _, _, d in col_peers])
-    psends = {k: remote(panel, band.at[row], pss.at[k], prs.at[k], d) for k, d in row_peers}
     own = pltpu.make_async_copy(panel, band.at[row], lsem.at[0])
-    for dx, dy in ((1, 0), (3, 0), (0, 1)):
-        psends[dx * NYL + dy].start()
     own.start()
 
     wacc[...] = jnp.zeros_like(wacc)
     lanes = lax.broadcasted_iota(I32, (T, T), 1)
     bands = lax.broadcasted_iota(I32, (COL_TILES, T), 0)
+    for copy in slots:
+        copy.wait()
 
     def some(b, per_context):
         await_counts(counts, held, cs, b)
@@ -122,27 +139,54 @@
         wacc[...] = per_word
         return per_context
 
-    per_context = lax.fori_loop(0, counts.shape[0] // GROUP, some, jnp.zeros((COL_TILES, T), I32))
+    per_context = lax.fori_loop(0, blocks, some, jnp.zeros((COL_TILES, T), I32))
     contexts[...] = per_context.astype(F32)
+    for d in range(N_COL):
+        words[d, 0:4, :] = wacc[pl.ds(4 * d, 4), :]
+        words[d, 4:8, :] = jnp.zeros((4, T), F32)
+    await_hails(everybody)
+
     csends = [remote(contexts, crecv.at[k], css.at[k], crs.at[k], d) for k, d in row_peers]
     for copy in csends:
         copy.start()
-    for d in range(N_COL):
-        words[d, 0:4, :] = wacc[pl.ds(4 * d, 4), :]
-        words[d, 4:8, :] = jnp.zeros((4, T), F32)
     wsends = [remote(words.at[p], wrecv.at[k], wss.at[k], wrs.at[k], d) for k, p, d in col_peers]
     for copy in wsends:
         copy.start()
-    for dx, dy in ((1, 1), (3, 1)):
-        psends[dx * NYL + dy].start()
+
+    psends = []
+
+    def pass_on(src, dst, device):
+        k = len(psends)
+        psends.append(remote(src, dst, pss.at[k], prs.at[k], device))
+        psends[k].start()
+
+    def to_right_and_left(first, second):
+        pass_on(first, first, {"x": right})
+        pass_on(second, second, {"x": left})
+
+    def relay(y):
+        to_right_and_left(
+            band.at[y * NX + left, pl.ds(0, HALF)], band.at[y * NX + right, pl.ds(HALF, HALF)]
+        )
+
+    pass_on(panel, band.at[row], {"yl": 1 - yl})
+    pass_on(panel, band.at[row], {"x": right})
+    pass_on(panel, band.at[row], {"x": left})
 
     for copy in csends:
         copy.wait_recv()
     contexts_sum = contexts[...]
     for k, _ in row_peers:
         contexts_sum = contexts_sum + crecv[k]
-    contexts_all[...] = contexts_sum
-    band_power = jnp.sum(powers_of(contexts_sum), keepdims=True)
+    powers = powers_of(contexts_sum)
+    band_power = jnp.sum(powers, keepdims=True)
+    context_log[...] = jnp.log(jnp.maximum(powers, 1.0))
+
+    for copy in psends[0:3]:
+        copy.wait_recv()
+    there = band.at[(1 - yl) * NX + x]
+    to_right_and_left(there, there)
+    relay(yl)
 
     for copy in wsends:
         copy.wait_recv()
@@ -154,14 +198,28 @@
     asends = [remote(mine, words_all.at[col], ass.at[k], ars.at[k], d) for k, _, d in col_peers]
     for copy in asends:
         copy.start()
-    for dx, dy in ((2, 0), (2, 1)):
-        psends[dx * NYL + dy].start()
     words_all[col] = mine[...]
+
+    def logs(b, carry):
+        for g in range(GROUP):
+            slot = b * GROUP + g
+            value = held[slot].astype(F32)
+            base[slot] = jnp.where(
+                value > 0.0, jnp.log(value) - context_log[pl.ds(cols[slot], 1), :], -1e30
+            )
+        return carry
+
+    lax.fori_loop(0, blocks // 2, logs, 0)
+    for copy in psends[3:5]:
+        copy.wait_recv()
+    relay(1 - yl)
+    lax.fori_loop(blocks // 2, blocks, logs, 0)
+
     for copy in asends:
         copy.wait()
-    for copy in csends + wsends:
+    for copy in csends + wsends + psends[0:5]:
         copy.wait_send()
-    for copy in psends.values():
+    for copy in psends[5:9]:
         copy.wait()
     own.wait()
 
@@ -170,39 +228,40 @@
     slots = counts.shape[0]
     return pl.pallas_call(
         totals_kernel,
-        in_specs=[SMEM, SMEM, ANY, ANY],
-        out_specs=[VMEM, VMEM, ANY, VMEM],
+        in_specs=[ANY, ANY, ANY, ANY],
+        out_specs=[VMEM, ANY, VMEM],
         out_shape=[
             jax.ShapeDtypeStruct((N_COL, 8, T), F32),
-            jax.ShapeDtypeStruct((COL_TILES, T), F32),
             jax.ShapeDtypeStruct((N_ROW, SHARE, T), BF16),
-            jax.ShapeDtypeStruct((slots, T, T), I32),
+            jax.ShapeDtypeStruct((slots, T, T), F32),
         ],
         scratch_shapes=[
+            pltpu.VMEM((slots, T, T), I32),
+            pltpu.SMEM((slots,), I32),
+            pltpu.SMEM((slots,), I32),
             pltpu.VMEM((T, ROW_TILES), F32),
             pltpu.VMEM((N_COL, 8, T), F32),
+            pltpu.VMEM((COL_TILES, T), F32),
             pltpu.VMEM((COL_TILES, T), F32),
             pltpu.VMEM((N_COL, 8, T), F32),
             pltpu.VMEM((N_ROW, COL_TILES, T), F32),
             pltpu.VMEM((8, T), F32),
             DMA((slots // GROUP,)),
             DMA((N_COL,)), DMA((N_COL,)), DMA((N_ROW,)), DMA((N_ROW,)),
-            DMA((N_COL,)), DMA((N_COL,)), DMA((N_ROW,)), DMA((N_ROW,)), DMA((1,)),
+            DMA((N_COL,)), DMA((N_COL,)), DMA((9,)), DMA((9,)), DMA((3,)),
         ],
         compiler_params=pltpu.CompilerParams(collective_id=0, has_side_effects=True, vmem_limit_bytes=16 << 20),
         name="totals",
     )(rows, cols, counts, panel)
 
 
-def word_kernel(rows, cols, counts, words_all, contexts_all, band, tiles, partial,
-                word_term, context_log):
+def word_kernel(rows, cols, base, words_all, band, tiles, partial, word_term):
     power = jnp.zeros((1, T), F32)
     for d in range(N_COL):
         word_term[pl.ds(4 * d, 4), :] = words_all[d, 0:4, :]
         power = power + words_all[d, 4:5, :]
     log_scale = jnp.log(power) - math.log(NEG_SAMPLES)
     word_term[...] = log_scale - jnp.log(jnp.maximum(word_term[...], 1.0))
-    context_log[...] = jnp.log(jnp.maximum(powers_of(contexts_all[...]), 1.0))
 
     def clear(t, carry):
         partial[t] = jnp.zeros((T, T), F32)
@@ -214,31 +273,29 @@
         for g in range(GROUP):
             slot = b * GROUP + g
             row, col = rows[slot], cols[slot]
-            value = counts[slot]
             per_word = jnp.take_along_axis(word_term[...], jnp.full((T, T), row, I32), axis=1)
-            pointwise = jnp.log(value.astype(F32)) + per_word - context_log[pl.ds(col, 1), :]
-            tile = jnp.where(value > 0, jnp.maximum(pointwise, 0.0), 0.0).astype(BF16)
+            tile = jnp.maximum(base[slot] + per_word, 0.0).astype(BF16)
             tiles[slot] = tile
             partial[row] += jnp.dot(tile, band[col], preferred_element_type=F32)
         return carry
 
-    lax.fori_loop(0, counts.shape[0] // GROUP, some, 0)
-
-
-def word_products(rows, cols, counts, words_all, contexts_all, band):
-    slots = counts.shape[0]
+    lax.fori_loop(0, base.shape[0] // GROUP, some, 0)
+
+
+def word_products(rows, cols, base, words_all, band):
+    slots = base.shape[0]
     return pl.pallas_call(
         word_kernel,
-        in_specs=[SMEM, SMEM, VMEM, VMEM, VMEM, VMEM],
+        in_specs=[SMEM, SMEM, VMEM, VMEM, VMEM],
         out_specs=[VMEM, VMEM],
-        scratch_shapes=[pltpu.VMEM((T, ROW_TILES), F32), pltpu.VMEM((COL_TILES, T), F32)],
+        scratch_shapes=[pltpu.VMEM((T, ROW_TILES), F32)],
         out_shape=[
             jax.ShapeDtypeStruct((slots, T, T), BF16),
             jax.ShapeDtypeStruct((ROW_TILES, T, T), F32),
         ],
         compiler_params=pltpu.CompilerParams(vmem_limit_bytes=28 << 20),
         name="word_products",
-    )(rows, cols, counts, words_all, contexts_all, band)
+    )(rows, cols, base, words_all, band)
 
 
 AWAY = (0, 1, 0)
@@ -260,8 +317,8 @@
 X_STEPS = lane_steps(NX // 2)
 
 
-def ring_sum(steps, length, y, raw, ready, ways, other_y, sendb, recvb, ysendb, yrecvb,
-             ss, rs, yss, yrs):
+def ring_sum(steps, length, y, raw, ready, ways, other_y, use, sendb, recvb,
+             ysendb, yrecvb, ss, rs, yss, yrs):
     trades, sends, traded = {}, {}, set()
 
     def trade(d):
@@ -315,9 +372,10 @@
         index, copy = sends[last, way, 2]
         copy.wait_recv()
         second = second + decode(recvb.at[index])
+    use(1, second)
     first = arrived(y)
     swap.wait_recv()
-    first = first + decode(yrecvb.at[end])
+    use(0, first + decode(yrecvb.at[end]))
 
     def drain():
         for _, copy in sends.values():
@@ -326,7 +384,7 @@
             copy.wait_send()
         swap.wait_send()
 
-    return first, second, drain
+    return drain
 
 
 def ring_scratch(steps, length):
@@ -361,20 +419,12 @@
         rows = pl.ds(part * HALF, HALF)
         return partial[lax.rem(z + d, NZ), h, c, rows, :] + sib[d * 2 + h, rows, :]
 
-    first, second, drain = ring_sum(Z_STEPS, length, yh, raw, ready, ways, other_y, *ring)
-    for part, total in enumerate((first, second)):
-        share[pl.ds(part * HALF, HALF), :] = total
-        for t in range(2):
-            mine[part * 2 + t] = total[t * T : (t + 1) * T].T.astype(BF16)
-
     pair = (pl.ds(0, 2), pl.ds(2, 2))
 
     def place(d, h, part):
         return everyone.at[lax.rem(z + d, NZ), h, c, pair[part]]
 
-    keep = pltpu.make_async_copy(mine, everyone.at[z, yh, c], ms.at[0])
-    keep.start()
-    gives, hands, passes = {}, [], {}
+    gives, hands, passes, keeps = {}, [], {}, []
 
     def hand(src, dst, k):
         copy = remote(src, dst, hss.at[k], hrs.at[k], other_core)
@@ -395,14 +445,19 @@
         gives[s, way, lane].start()
 
     own = (mine.at[pair[0]], mine.at[pair[1]])
-    along_y(own[0], place(0, yh, 0), NZ)
-    for way in range(2):
-        give(0, way, 2, own[1])
-    for way in range(2):
-        give(0, way, 0, own[0])
-    along_y(own[1], place(0, yh, 1), 0)
-    hand(own[0], place(0, yh, 0), 0)
-    hand(own[1], place(0, yh, 1), 2 * NZ)
+
+    def use(part, total):
+        for t in range(2):
+            mine[part * 2 + t] = total[t * T : (t + 1) * T].T.astype(BF16)
+        along_y(own[part], place(0, yh, part), 0 if part else NZ)
+        for way in range(2):
+            give(0, way, 2 if part else 0, own[part])
+        hand(own[part], place(0, yh, part), 2 * NZ if part else 0)
+        keeps.append(pltpu.make_async_copy(own[part], place(0, yh, part), ms.at[part]))
+        keeps[-1].start()
+        share[pl.ds(part * HALF, HALF), :] = total
+
+    drain = ring_sum(Z_STEPS, length, yh, raw, ready, ways, other_y, use, *ring)
     passes[NZ].wait_recv()
     for way in range(2):
         give(0, way, 1)
@@ -436,7 +491,8 @@
     for copy in list(gives.values()) + list(passes.values()) + list(swaps.values()):
         copy.wait_send()
     drain()
-    keep.wait()
+    for copy in keeps:
+        copy.wait()
 
 
 def word_panel_sum(partial):
@@ -452,7 +508,7 @@
             pltpu.VMEM((2 * NZ, SHARE, T), F32),
             pltpu.VMEM((4, T, T), BF16),
             DMA((2 * NZ,)), DMA((2 * NZ,)), DMA((3 * NZ,)), DMA((3 * NZ,)),
-            DMA((4 * NZ,)), DMA((4 * NZ,)), DMA((NZ + 1,)), DMA((NZ + 1,)), DMA((1,)),
+            DMA((4 * NZ,)), DMA((4 * NZ,)), DMA((NZ + 1,)), DMA((NZ + 1,)), DMA((2,)),
             *ring_scratch(Z_STEPS, NZ // 2),
         ],
         compiler_params=pltpu.CompilerParams(collective_id=1, has_side_effects=True, vmem_limit_bytes=16 << 20),
@@ -497,14 +553,12 @@
     def raw(d, h, part):
         return partial[h, lax.rem(x + d, NX), pl.ds(part * HALF, HALF), :]
 
-    first, second, drain = ring_sum(
-        X_STEPS, NX // 2, yl, raw, lambda d: None, ways, other_y, *ring
-    )
-    for part, total in enumerate((first, second)):
+    def use(part, total):
         total = total * (1.0 / T)
         for t in range(2):
             share[pl.ds(part * HALF + t * T, T), :] = total[t * T : (t + 1) * T].T
-    drain()
+
+    ring_sum(X_STEPS, NX // 2, yl, raw, lambda d: None, ways, other_y, use, *ring)()
 
 
 def context_panel_sum(partial):
@@ -521,10 +575,10 @@
 
 def shards(tile_counts, tile_rows, tile_cols, panel):
     counts, rows, cols = tile_counts[0, 0], tile_rows[0, 0], tile_cols[0, 0]
-    counts = pltpu.with_memory_space_constraint(counts, pltpu.HBM)
-    words_all, contexts_all, band, held = totals(rows, cols, counts, panel)
+    far = [pltpu.with_memory_space_constraint(a, pltpu.HBM) for a in (rows, cols, counts, panel)]
+    words_all, band, base = totals(*far)
     band = band.reshape(COL_TILES, T, T)
-    tiles, partial = word_products(rows, cols, held, words_all, contexts_all, band)
+    tiles, partial = word_products(rows, cols, base, words_all, band)
     share, everyone = word_panel_sum(partial.reshape(NZ, NYH, NC, SHARE, T))
     rounded = everyone.reshape(ROW_TILES, T, T)
     context_partial, share = context_products(rows, cols, tiles, rounded, share)

time: 122 us -> 110 us (0.902); the launches traced: 121 us -> 110 us
  Pallas kernels: 117 us -> 109 us
  local copies, waits for them, and re-layouts: 2.98 us -> 0.71 us
    pallas_call x2, Pallas kernels: 42.6 us -> 35.6 us  [the longest x1 28.7 us: totals(): pl.pallas_call(totals_kernel, in_specs=[ANY, ANY, ANY, ANY], out_specs=[V...]
    unnamed x11 -> x5, local copies, waits for them, and re-layouts: 2.98 us -> 0.71 us
    pallas_call x1, Pallas kernels: 53.2 us -> 51.7 us  [word_panel_sum(): pl.pallas_call(word_panel_kernel, in_specs=[VMEM], out_specs=[VMEM, ANY],...]
where the time goes in v4:
time: 110 us
  Pallas kernels  109 us (99%)
    pallas_call x1, Pallas kernels, word_panel_sum(): pl.pallas_call(word_panel_kernel, in_specs=[VMEM], out_specs=[VMEM, ANY],...  51.7 us
    pallas_call x1, Pallas kernels, totals(): pl.pallas_call(totals_kernel, in_specs=[ANY, ANY, ANY, ANY], out_specs=[V...  28.7 us
    pallas_call x1, Pallas kernels, context_panel_sum(): pl.pallas_call(context_panel_kernel, in_specs=[VMEM], out_specs=VMEM, out...  17.1 us
    pallas_call x1, Pallas kernels, word_products(): pl.pallas_call(word_kernel, in_specs=[SMEM, SMEM, VMEM, VMEM, VMEM], out_...  6.9 us
    pallas_call x1, Pallas kernels, context_products(): pl.pallas_call(context_kernel, in_specs=[SMEM, SMEM, VMEM, VMEM, VMEM], o...  4.42 us

profile of v4, /device:TPU:8, one launch (start us, length us, event | category | flops | bytes accessed | tf_op | source)
XLA Modules:
  0.0 110.2 jit_solution(8907340407893041806)
XLA Ops:
  0.6 0.0 copy-start.1
  0.6 0.0 copy-start
  0.7 28.7 %totals.1 = (f32[32,8,128]{2,1,0:T(8,128)S(1)}, bf16[8,512,128]{2,1,0:T(8,128)(2,1)S(1)}, f32[160,128,128]{2,1,0:T(8,128)S(1)}) custom-call(s32[160]{0:T(256)} %bitcast.11, s32[160]{0:T(256)} %bitcast.14, s32[160,128,128]{2,1,0:T(8,128)} %bitcast.17, bf16[512,128]{1,0:T(8,128)(2,1)} %panel.1), custom_call_target="tpu_custom_call" | custom-call | tf_op jit(solution)/shard_map/totals/pallas_call | solution.py:229
  29.3 0.0 copy-done.1
  29.3 0.0 copy-done
  29.4 6.9 %word_products.1 = (bf16[160,128,128]{2,1,0:T(8,128)(2,1)S(1)}, f32[128,128,128]{2,1,0:T(8,128)S(1)}) custom-call(s32[160]{0:T(256)S(1)} %bitcast.12, s32[160]{0:T(256)S(1)} %bitcast.15, f32[160,128,128]{2,1,0:T(8,128)S(1)} %get-tuple-element.11.base, f32[32,8,128]{2,1,0:T(8,128)S(1)} %get-tuple-element.12.words_all, bf16[32,128,128]{2,1,0:T(8,128)(2,1)S(1)} %bitcast.10), custom_call_target="tpu_custom_call" | custom-call | tf_op jit(solution)/shard_map/word_products/pallas_call | solution.py:287
  36.3 51.7 %word_panel_sum.1 = (f32[512,128]{1,0:T(8,128)S(1)}, bf16[8,2,2,4,128,128]{5,4,3,2,1,0:T(8,128)(2,1)S(1)}) custom-call(f32[8,2,2,512,128]{4,3,2,1,0:T(8,128)S(1)} %bitcast.7), custom_call_target="tpu_custom_call" | custom-call | tf_op jit(solution)/shard_map/word_panel_sum/pallas_call | solution.py:499
  88.0 4.4 %context_products.1 = (f32[32,128,128]{2,1,0:T(8,128)S(1)}, f32[512,128]{1,0:T(8,128)}) custom-call(s32[160]{0:T(256)S(1)} %bitcast.13, s32[160]{0:T(256)S(1)} %bitcast.16, bf16[160,128,128]{2,1,0:T(8,128)(2,1)S(1)} %get-tuple-element.14.tiles, bf16[128,128,128]{2,1,0:T(8,128)(2,1)S(1)} %bitcast.8, f32[512,128]{1,0:T(8,128)S(1)} %get-tuple-element.17.share), custom_call_target="tpu_custom_call" | custom-call | tf_op jit(solution)/shard_map/context_products/pallas_call | solution.py:534
  92.4 17.1 %context_panel_sum.1 = f32[512,128]{1,0:T(8,128)S(1)} custom-call(f32[2,4,512,128]{3,2,1,0:T(8,128)S(1)} %bitcast.9), custom_call_target="tpu_custom_call" | custom-call | tf_op jit(solution)/shard_map/context_panel_sum/pallas_call | solution.py:565
  109.5 0.7 copy.7
Async XLA Ops:
  0.6 28.7 %copy-start.1 = (s32[1,1,160]{2,1,0:T(1,128)S(1)}, s32[1,1,160]{2,1,0:T(1,128)}, u32[]{:S(2)}) copy-start(s32[1,1,160]{2,1,0:T(1,128)} %param.6) | copy-start | bytes 1924
  0.6 28.7 %copy-start = (s32[1,1,160]{2,1,0:T(1,128)S(1)}, s32[1,1,160]{2,1,0:T(1,128)}, u32[]{:S(2)}) copy-start(s32[1,1,160]{2,1,0:T(1,128)} %param.5) | copy-start | bytes 1924

commit v5 on v4

--- a/solution.py
+++ b/solution.py
@@ -63,6 +63,7 @@
 
 
 GROUP = 16
+PART = T // NZ
 
 
 def powers_of(totals):
@@ -85,29 +86,23 @@
 
 
 def totals_kernel(rows_in, cols_in, counts, panel, words_all, band, base,
-                  held, rows, cols, wacc, words, contexts, context_log, wrecv, crecv, mine,
-                  cs, wss, wrs, css, crs, ass, ars, pss, prs, lsem):
+                  held, rows, cols, wacc, contexts, context_log, wrecv, crecv, mine, qrecv,
+                  cs, wss, wrs, css, crs, qss, qrs, ass, ars, pss, prs, lsem):
     x, yl = lax.axis_index("x"), lax.axis_index("yl")
     z, yh, c = lax.axis_index("z"), lax.axis_index("yh"), lax.axis_index("core")
     blocks = counts.shape[0] // GROUP
     row = yl * NX + x
-    col = (z * NYH + yh) * NC + c
     right, left = lax.rem(x + 1, NX), lax.rem(x + NX - 1, NX)
     row_peers = [
         (dx * NYL + dy, {"x": lax.rem(x + dx, NX), "yl": lax.rem(yl + dy, NYL)})
         for dx in range(NX) for dy in range(NYL) if dx or dy
     ]
-    col_peers = []
-    for dz in (4, 3, 5, 2, 6, 1, 7, 0):
-        for dy in (1, 0):
-            for dc in range(NC):
-                if dz or dy or dc:
-                    pz, py, pc = lax.rem(z + dz, NZ), lax.rem(yh + dy, NYH), lax.rem(c + dc, NC)
-                    col_peers.append(
-                        ((dz * NYH + dy) * NC + dc, (pz * NYH + py) * NC + pc,
-                         {"z": pz, "yh": py, "core": pc})
-                    )
-    everybody = [d for _, d in row_peers] + [d for _, _, d in col_peers]
+    z_peers = [(dz, lax.rem(z + dz, NZ)) for dz in (4, 3, 5, 2, 6, 1, 7)]
+    quad = [
+        (dy * NC + dc, {"yh": lax.rem(yh + dy, NYH), "core": lax.rem(c + dc, NC)})
+        for dy, dc in ((1, 0), (1, 1), (0, 1))
+    ]
+    everybody = [d for _, d in row_peers] + [{"z": p} for _, p in z_peers] + [d for _, d in quad]
     hail(everybody)
     slots = [
         pltpu.make_async_copy(rows_in, rows, lsem.at[1]),
@@ -141,15 +136,15 @@
 
     per_context = lax.fori_loop(0, blocks, some, jnp.zeros((COL_TILES, T), I32))
     contexts[...] = per_context.astype(F32)
-    for d in range(N_COL):
-        words[d, 0:4, :] = wacc[pl.ds(4 * d, 4), :]
-        words[d, 4:8, :] = jnp.zeros((4, T), F32)
     await_hails(everybody)
 
     csends = [remote(contexts, crecv.at[k], css.at[k], crs.at[k], d) for k, d in row_peers]
     for copy in csends:
         copy.start()
-    wsends = [remote(words.at[p], wrecv.at[k], wss.at[k], wrs.at[k], d) for k, p, d in col_peers]
+    wsends = [
+        remote(wacc.at[pl.ds(pl.multiple_of(p * PART, PART), PART)], wrecv.at[k], wss.at[k], wrs.at[k], {"z": p})
+        for k, p in z_peers
+    ]
     for copy in wsends:
         copy.start()
 
@@ -190,15 +185,25 @@
 
     for copy in wsends:
         copy.wait_recv()
-    words_sum = words[col]
-    for k, _, _ in col_peers:
+    words_sum = wacc[pl.ds(pl.multiple_of(z * PART, PART), PART), :]
+    for k, _ in z_peers:
         words_sum = words_sum + wrecv[k]
-    at = lax.broadcasted_iota(I32, (8, T), 0)
-    mine[...] = jnp.where(at == 4, jnp.broadcast_to(band_power, (8, T)), words_sum)
-    asends = [remote(mine, words_all.at[col], ass.at[k], ars.at[k], d) for k, _, d in col_peers]
+    mine[pl.ds(0, PART), :] = words_sum
+    mine[pl.ds(PART, 8), :] = jnp.broadcast_to(band_power, (8, T))
+    qsends = [remote(mine, qrecv.at[k], qss.at[k], qrs.at[k], d) for k, d in quad]
+    for copy in qsends:
+        copy.start()
+    for copy in qsends:
+        copy.wait_recv()
+    total = mine[...]
+    for k, _ in quad:
+        total = total + qrecv[k]
+    words_all[z] = total
+    asends = [
+        remote(words_all.at[z], words_all.at[z], ass.at[k], ars.at[k], {"z": p}) for k, p in z_peers
+    ]
     for copy in asends:
         copy.start()
-    words_all[col] = mine[...]
 
     def logs(b, carry):
         for g in range(GROUP):
@@ -217,7 +222,7 @@
 
     for copy in asends:
         copy.wait()
-    for copy in csends + wsends + psends[0:5]:
+    for copy in csends + wsends + qsends + psends[0:5]:
         copy.wait_send()
     for copy in psends[5:9]:
         copy.wait()
@@ -231,7 +236,7 @@
         in_specs=[ANY, ANY, ANY, ANY],
         out_specs=[VMEM, ANY, VMEM],
         out_shape=[
-            jax.ShapeDtypeStruct((N_COL, 8, T), F32),
+            jax.ShapeDtypeStruct((NZ, PART + 8, T), F32),
             jax.ShapeDtypeStruct((N_ROW, SHARE, T), BF16),
             jax.ShapeDtypeStruct((slots, T, T), F32),
         ],
@@ -240,15 +245,15 @@
             pltpu.SMEM((slots,), I32),
             pltpu.SMEM((slots,), I32),
             pltpu.VMEM((T, ROW_TILES), F32),
-            pltpu.VMEM((N_COL, 8, T), F32),
             pltpu.VMEM((COL_TILES, T), F32),
             pltpu.VMEM((COL_TILES, T), F32),
-            pltpu.VMEM((N_COL, 8, T), F32),
+            pltpu.VMEM((NZ, PART, T), F32),
             pltpu.VMEM((N_ROW, COL_TILES, T), F32),
-            pltpu.VMEM((8, T), F32),
+            pltpu.VMEM((PART + 8, T), F32),
+            pltpu.VMEM((NYH * NC, PART + 8, T), F32),
             DMA((slots // GROUP,)),
-            DMA((N_COL,)), DMA((N_COL,)), DMA((N_ROW,)), DMA((N_ROW,)),
-            DMA((N_COL,)), DMA((N_COL,)), DMA((9,)), DMA((9,)), DMA((3,)),
+            DMA((NZ,)), DMA((NZ,)), DMA((N_ROW,)), DMA((N_ROW,)), DMA((NYH * NC,)), DMA((NYH * NC,)),
+            DMA((NZ,)), DMA((NZ,)), DMA((9,)), DMA((9,)), DMA((3,)),
         ],
         compiler_params=pltpu.CompilerParams(collective_id=0, has_side_effects=True, vmem_limit_bytes=16 << 20),
         name="totals",
@@ -257,9 +262,9 @@
 
 def word_kernel(rows, cols, base, words_all, band, tiles, partial, word_term):
     power = jnp.zeros((1, T), F32)
-    for d in range(N_COL):
-        word_term[pl.ds(4 * d, 4), :] = words_all[d, 0:4, :]
-        power = power + words_all[d, 4:5, :]
+    for d in range(NZ):
+        word_term[pl.ds(d * PART, PART), :] = words_all[d, 0:PART, :]
+        power = power + words_all[d, PART : PART + 1, :]
     log_scale = jnp.log(power) - math.log(NEG_SAMPLES)
     word_term[...] = log_scale - jnp.log(jnp.maximum(word_term[...], 1.0))
 
@@ -300,32 +305,29 @@
 
 AWAY = (0, 1, 0)
 
-
-def lane_steps(length):
-    steps = []
-    for s in range(length):
-        for lanes in ((0, 1), (2,)):
-            for far in (False, True):
-                for lane in lanes:
-                    for way in range(2):
-                        if (way == AWAY[lane]) == far and (far or s):
-                            steps.append((s, way, lane))
-    return steps
-
-
-Z_STEPS = lane_steps(NZ // 2)
-X_STEPS = lane_steps(NX // 2)
+Z_STEPS = (
+    4, (0, 0, 0), (0, 1, 1), 3, 5,
+    (1, 1, 0), (1, 0, 1), (1, 0, 0), (1, 1, 1), (0, 0, 2), 2, 6,
+    (2, 1, 0), (2, 0, 1), (2, 0, 0), (2, 1, 1), (1, 1, 2), (1, 0, 2), 1, 7,
+    (3, 1, 0), (3, 0, 1), (3, 0, 0), (3, 1, 1), 0, (2, 1, 2), (2, 0, 2), None,
+    (3, 1, 2), (3, 0, 2),
+)
+X_STEPS = (
+    2, (0, 0, 0), (0, 1, 1), 1, 3,
+    (1, 1, 0), (1, 0, 1), (0, 0, 2), (1, 0, 0), (1, 1, 1), 0, None,
+    (1, 1, 2), (1, 0, 2),
+)
 
 
 def ring_sum(steps, length, y, raw, ready, ways, other_y, use, sendb, recvb,
              ysendb, yrecvb, ss, rs, yss, yrs):
     trades, sends, traded = {}, {}, set()
-
-    def trade(d):
-        ready(d)
-        encode(raw(d, 1 - y, 1), ysendb.at[d])
-        trades[d] = remote(ysendb.at[d], yrecvb.at[d], yss.at[d], yrs.at[d], other_y)
-        trades[d].start()
+    last, end = length - 1, 2 * length
+
+    def exchange(value, k):
+        encode(value, ysendb.at[k])
+        trades[k] = remote(ysendb.at[k], yrecvb.at[k], yss.at[k], yrs.at[k], other_y)
+        trades[k].start()
 
     def term(d, lane):
         if lane < 2:
@@ -335,27 +337,6 @@
             traded.add(d)
         return raw(d, y, 1) + decode(yrecvb.at[d])
 
-    trade(length)
-    for n, (s, way, lane) in enumerate(steps):
-        if lane == 2 and (n == 0 or steps[n - 1][2] != 2):
-            for d in sorted({length - s - 1, (length + s + 1) % (2 * length)}):
-                trade(d)
-        d = length - s if way == 0 else length + s
-        value = term(d, lane)
-        if (s - 1, way, lane) in sends:
-            index, before = sends[s - 1, way, lane]
-            before.wait_recv()
-            value = value + decode(recvb.at[index])
-        encode(value, sendb.at[n])
-        copy = remote(sendb.at[n], recvb.at[n], ss.at[n], rs.at[n], ways[way])
-        copy.start()
-        sends[s, way, lane] = (n, copy)
-
-    last = length - 1
-    for lane in (0, 1):
-        for way in range(2):
-            sends[last, way, lane][1].wait_recv()
-
     def arrived(h):
         value = raw(0, h, 0)
         for way in range(2):
@@ -363,32 +344,49 @@
             value = value + decode(recvb.at[first + h * (second - first)])
         return value
 
-    end = 2 * length
-    encode(arrived(1 - y), ysendb.at[end])
-    swap = remote(ysendb.at[end], yrecvb.at[end], yss.at[end], yrs.at[end], other_y)
-    swap.start()
+    for step in steps:
+        if step is None:
+            for lane in (0, 1):
+                for way in range(2):
+                    sends[last, way, lane][1].wait_recv()
+            exchange(arrived(1 - y), end)
+        elif isinstance(step, int):
+            ready(step)
+            exchange(raw(step, 1 - y, 1), step)
+        else:
+            s, way, lane = step
+            value = term(length - s if way == 0 else length + s, lane)
+            if (s - 1, way, lane) in sends:
+                index, before = sends[s - 1, way, lane]
+                before.wait_recv()
+                value = value + decode(recvb.at[index])
+            n = len(sends)
+            encode(value, sendb.at[n])
+            copy = remote(sendb.at[n], recvb.at[n], ss.at[n], rs.at[n], ways[way])
+            copy.start()
+            sends[step] = (n, copy)
+
+    first = arrived(y)
+    trades[end].wait_recv()
+    use(0, first + decode(yrecvb.at[end]))
     second = term(0, 2)
     for way in range(2):
         index, copy = sends[last, way, 2]
         copy.wait_recv()
         second = second + decode(recvb.at[index])
     use(1, second)
-    first = arrived(y)
-    swap.wait_recv()
-    use(0, first + decode(yrecvb.at[end]))
 
     def drain():
         for _, copy in sends.values():
             copy.wait_send()
         for copy in trades.values():
             copy.wait_send()
-        swap.wait_send()
 
     return drain
 
 
 def ring_scratch(steps, length):
-    n, y = len(steps), 2 * length + 1
+    n, y = sum(isinstance(step, tuple) for step in steps), 2 * length + 1
     return [
         pltpu.VMEM((n, CODE, T), I16), pltpu.VMEM((n, CODE, T), I16),
         pltpu.VMEM((y, CODE, T), I16), pltpu.VMEM((y, CODE, T), I16),
@@ -465,7 +463,7 @@
     due = [0]
     for s in range(1, length + 1):
         came = []
-        for lane in (2, 0, 1):
+        for lane in (0, 2, 1) if s == 1 else (2, 0, 1):
             for way in range(2):
                 if (s - 1, way, lane) not in gives:
                     continue
@@ -516,17 +514,20 @@
     )(partial)
 
 
-def context_kernel(rows, cols, tiles, rounded, share, partial, share_out):
+def context_kernel(rows, cols, tiles, rounded, share, partial, share_out, odd):
     share_out[...] = share[...]
-    partial[...] = jnp.zeros_like(partial)
+    sums = (partial, odd)
+    for ref in sums:
+        ref[...] = jnp.zeros_like(ref)
 
     def some(b, carry):
         for g in range(GROUP):
             slot = b * GROUP + g
-            partial[cols[slot]] += jnp.dot(rounded[rows[slot]], tiles[slot], preferred_element_type=F32)
+            sums[g % 2][cols[slot]] += jnp.dot(rounded[rows[slot]], tiles[slot], preferred_element_type=F32)
         return carry
 
     lax.fori_loop(0, tiles.shape[0] // GROUP, some, 0)
+    partial[...] += odd[...]
 
 
 def context_products(rows, cols, tiles, rounded, share):
@@ -539,6 +540,7 @@
             jax.ShapeDtypeStruct((COL_TILES, T, T), F32),
             jax.ShapeDtypeStruct((SHARE, T), F32),
         ],
+        scratch_shapes=[pltpu.VMEM((COL_TILES, T, T), F32)],
         compiler_params=pltpu.CompilerParams(vmem_limit_bytes=16 << 20),
         name="context_products",
     )(rows, cols, tiles, rounded, share)

time: 110 us -> 104 us (0.945)
  Pallas kernels: 109 us -> 103 us
    pallas_call x1, Pallas kernels: 51.7 us -> 49.3 us  [word_panel_sum(): pl.pallas_call(word_panel_kernel, in_specs=[VMEM], out_specs=[VMEM, ANY],...]
    pallas_call x1, Pallas kernels: 17.1 us -> 15 us  [context_panel_sum(): pl.pallas_call(context_panel_kernel, in_specs=[VMEM], out_specs=VMEM, out...]
    pallas_call x1, Pallas kernels: 28.7 us -> 26.8 us  [totals(): pl.pallas_call(totals_kernel, in_specs=[ANY, ANY, ANY, ANY], out_specs=[V...]
where the time goes in v5:
time: 104 us
  Pallas kernels  103 us (99%)
    pallas_call x1, Pallas kernels, word_panel_sum(): pl.pallas_call(word_panel_kernel, in_specs=[VMEM], out_specs=[VMEM, ANY],...  49.3 us
    pallas_call x1, Pallas kernels, totals(): pl.pallas_call(totals_kernel, in_specs=[ANY, ANY, ANY, ANY], out_specs=[V...  26.8 us
    pallas_call x1, Pallas kernels, context_panel_sum(): pl.pallas_call(context_panel_kernel, in_specs=[VMEM], out_specs=VMEM, out...  15 us
    pallas_call x1, Pallas kernels, word_products(): pl.pallas_call(word_kernel, in_specs=[SMEM, SMEM, VMEM, VMEM, VMEM], out_...  6.87 us
    pallas_call x1, Pallas kernels, context_products(): pl.pallas_call(context_kernel, in_specs=[SMEM, SMEM, VMEM, VMEM, VMEM], o...  4.59 us

profile of v5, /device:TPU:8, one launch (start us, length us, event | category | flops | bytes accessed | tf_op | source)
XLA Modules:
  0.0 104.0 jit_solution(8417837663439001050)
XLA Ops:
  0.6 0.0 copy-start.1
  0.6 0.0 copy-start
  0.7 26.8 %totals.1 = (f32[8,24,128]{2,1,0:T(8,128)S(1)}, bf16[8,512,128]{2,1,0:T(8,128)(2,1)S(1)}, f32[160,128,128]{2,1,0:T(8,128)S(1)}) custom-call(s32[160]{0:T(256)} %bitcast.11, s32[160]{0:T(256)} %bitcast.14, s32[160,128,128]{2,1,0:T(8,128)} %bitcast.17, bf16[512,128]{1,0:T(8,128)(2,1)} %panel.1), custom_call_target="tpu_custom_call" | custom-call | tf_op jit(solution)/shard_map/totals/pallas_call | solution.py:234
  27.5 0.0 copy-done.1
  27.5 0.0 copy-done
  27.5 6.9 %word_products.1 = (bf16[160,128,128]{2,1,0:T(8,128)(2,1)S(1)}, f32[128,128,128]{2,1,0:T(8,128)S(1)}) custom-call(s32[160]{0:T(256)S(1)} %bitcast.12, s32[160]{0:T(256)S(1)} %bitcast.15, f32[160,128,128]{2,1,0:T(8,128)S(1)} %get-tuple-element.11.base, f32[8,24,128]{2,1,0:T(8,128)S(1)} %get-tuple-element.12.words_all, bf16[32,128,128]{2,1,0:T(8,128)(2,1)S(1)} %bitcast.10), custom_call_target="tpu_custom_call" | custom-call | tf_op jit(solution)/shard_map/word_products/pallas_call | solution.py:292
  34.4 49.3 %word_panel_sum.1 = (f32[512,128]{1,0:T(8,128)S(1)}, bf16[8,2,2,4,128,128]{5,4,3,2,1,0:T(8,128)(2,1)S(1)}) custom-call(f32[8,2,2,512,128]{4,3,2,1,0:T(8,128)S(1)} %bitcast.7), custom_call_target="tpu_custom_call" | custom-call | tf_op jit(solution)/shard_map/word_panel_sum/pallas_call | solution.py:497
  83.7 4.6 %context_products.1 = (f32[32,128,128]{2,1,0:T(8,128)S(1)}, f32[512,128]{1,0:T(8,128)}) custom-call(s32[160]{0:T(256)S(1)} %bitcast.13, s32[160]{0:T(256)S(1)} %bitcast.16, bf16[160,128,128]{2,1,0:T(8,128)(2,1)S(1)} %get-tuple-element.14.tiles, bf16[128,128,128]{2,1,0:T(8,128)(2,1)S(1)} %bitcast.8, f32[512,128]{1,0:T(8,128)S(1)} %get-tuple-element.17.share), custom_call_target="tpu_custom_call" | custom-call | tf_op jit(solution)/shard_map/context_products/pallas_call | solution.py:535
  88.3 15.0 %context_panel_sum.1 = f32[512,128]{1,0:T(8,128)S(1)} custom-call(f32[2,4,512,128]{3,2,1,0:T(8,128)S(1)} %bitcast.9), custom_call_target="tpu_custom_call" | custom-call | tf_op jit(solution)/shard_map/context_panel_sum/pallas_call | solution.py:567
  103.3 0.7 copy.7
Async XLA Ops:
  0.6 26.9 %copy-start.1 = (s32[1,1,160]{2,1,0:T(1,128)S(1)}, s32[1,1,160]{2,1,0:T(1,128)}, u32[]{:S(2)}) copy-start(s32[1,1,160]{2,1,0:T(1,128)} %param.6) | copy-start | bytes 1924
  0.6 26.9 %copy-start = (s32[1,1,160]{2,1,0:T(1,128)S(1)}, s32[1,1,160]{2,1,0:T(1,128)}, u32[]{:S(2)}) copy-start(s32[1,1,160]{2,1,0:T(1,128)} %param.5) | copy-start | bytes 1924

commit v6 on v5

--- a/solution.py
+++ b/solution.py
@@ -85,8 +85,8 @@
     pltpu.make_async_copy(counts.at[part], held.at[part], sem.at[b]).wait()
 
 
-def totals_kernel(rows_in, cols_in, counts, panel, words_all, band, base,
-                  held, rows, cols, wacc, contexts, context_log, wrecv, crecv, mine, qrecv,
+def totals_kernel(rows_in, cols_in, counts, panel_in, words_all, band, base, cleared,
+                  brought, panel, held, rows, cols, wacc, contexts, context_log, wrecv, crecv, mine, qrecv,
                   cs, wss, wrs, css, crs, qss, qrs, ass, ars, pss, prs, lsem):
     x, yl = lax.axis_index("x"), lax.axis_index("yl")
     z, yh, c = lax.axis_index("z"), lax.axis_index("yh"), lax.axis_index("core")
@@ -103,14 +103,20 @@
         for dy, dc in ((1, 0), (1, 1), (0, 1))
     ]
     everybody = [d for _, d in row_peers] + [{"z": p} for _, p in z_peers] + [d for _, d in quad]
-    hail(everybody)
     slots = [
         pltpu.make_async_copy(rows_in, rows, lsem.at[1]),
         pltpu.make_async_copy(cols_in, cols, lsem.at[2]),
     ]
+    bring = pltpu.make_async_copy(panel_in, brought, lsem.at[3])
     for copy in slots:
         copy.start()
     load_counts(counts, held, cs)
+    bring.start()
+    hail(everybody)
+    bring.wait()
+    for t in range(4):
+        tile = pl.ds(t * T, T)
+        panel[tile, :] = brought[tile, :].astype(F32).T.astype(BF16)
     own = pltpu.make_async_copy(panel, band.at[row], lsem.at[0])
     own.start()
 
@@ -168,6 +174,11 @@
     pass_on(panel, band.at[row], {"x": right})
     pass_on(panel, band.at[row], {"x": left})
 
+    def clear(t, carry):
+        cleared[t] = jnp.zeros((T, T), F32)
+        return carry
+
+    lax.fori_loop(0, ROW_TILES, clear, 0, unroll=4)
     for copy in csends:
         copy.wait_recv()
     contexts_sum = contexts[...]
@@ -193,6 +204,18 @@
     qsends = [remote(mine, qrecv.at[k], qss.at[k], qrs.at[k], d) for k, d in quad]
     for copy in qsends:
         copy.start()
+
+    def logs(b, carry):
+        for g in range(GROUP):
+            slot = b * GROUP + g
+            value = held[slot].astype(F32)
+            term = jnp.where(
+                value > 0.0, jnp.log(value) - context_log[pl.ds(cols[slot], 1), :], -1e30
+            )
+            base[slot] = term.T
+        return carry
+
+    lax.fori_loop(0, blocks // 2, logs, 0)
     for copy in qsends:
         copy.wait_recv()
     total = mine[...]
@@ -205,20 +228,10 @@
     for copy in asends:
         copy.start()
 
-    def logs(b, carry):
-        for g in range(GROUP):
-            slot = b * GROUP + g
-            value = held[slot].astype(F32)
-            base[slot] = jnp.where(
-                value > 0.0, jnp.log(value) - context_log[pl.ds(cols[slot], 1), :], -1e30
-            )
-        return carry
-
-    lax.fori_loop(0, blocks // 2, logs, 0)
+    lax.fori_loop(blocks // 2, blocks, logs, 0)
     for copy in psends[3:5]:
         copy.wait_recv()
     relay(1 - yl)
-    lax.fori_loop(blocks // 2, blocks, logs, 0)
 
     for copy in asends:
         copy.wait()
@@ -234,13 +247,16 @@
     return pl.pallas_call(
         totals_kernel,
         in_specs=[ANY, ANY, ANY, ANY],
-        out_specs=[VMEM, ANY, VMEM],
+        out_specs=[VMEM, ANY, VMEM, VMEM],
         out_shape=[
             jax.ShapeDtypeStruct((NZ, PART + 8, T), F32),
             jax.ShapeDtypeStruct((N_ROW, SHARE, T), BF16),
             jax.ShapeDtypeStruct((slots, T, T), F32),
+            jax.ShapeDtypeStruct((ROW_TILES, T, T), F32),
         ],
         scratch_shapes=[
+            pltpu.VMEM((SHARE, T), BF16),
+            pltpu.VMEM((SHARE, T), BF16),
             pltpu.VMEM((slots, T, T), I32),
             pltpu.SMEM((slots,), I32),
             pltpu.SMEM((slots,), I32),
@@ -253,60 +269,54 @@
             pltpu.VMEM((NYH * NC, PART + 8, T), F32),
             DMA((slots // GROUP,)),
             DMA((NZ,)), DMA((NZ,)), DMA((N_ROW,)), DMA((N_ROW,)), DMA((NYH * NC,)), DMA((NYH * NC,)),
-            DMA((NZ,)), DMA((NZ,)), DMA((9,)), DMA((9,)), DMA((3,)),
+            DMA((NZ,)), DMA((NZ,)), DMA((9,)), DMA((9,)), DMA((4,)),
         ],
         compiler_params=pltpu.CompilerParams(collective_id=0, has_side_effects=True, vmem_limit_bytes=16 << 20),
         name="totals",
     )(rows, cols, counts, panel)
 
 
-def word_kernel(rows, cols, base, words_all, band, tiles, partial, word_term):
+def word_kernel(rows, cols, base, words_all, band, cleared, tiles, partial, words, word_term):
     power = jnp.zeros((1, T), F32)
     for d in range(NZ):
-        word_term[pl.ds(d * PART, PART), :] = words_all[d, 0:PART, :]
+        words[pl.ds(d * PART, PART), :] = words_all[d, 0:PART, :]
         power = power + words_all[d, PART : PART + 1, :]
     log_scale = jnp.log(power) - math.log(NEG_SAMPLES)
-    word_term[...] = log_scale - jnp.log(jnp.maximum(word_term[...], 1.0))
-
-    def clear(t, carry):
-        partial[t] = jnp.zeros((T, T), F32)
-        return carry
-
-    lax.fori_loop(0, ROW_TILES, clear, 0, unroll=4)
+    word_term[...] = (log_scale - jnp.log(jnp.maximum(words[...], 1.0))).T
 
     def some(b, carry):
         for g in range(GROUP):
             slot = b * GROUP + g
             row, col = rows[slot], cols[slot]
-            per_word = jnp.take_along_axis(word_term[...], jnp.full((T, T), row, I32), axis=1)
-            tile = jnp.maximum(base[slot] + per_word, 0.0).astype(BF16)
+            tile = jnp.maximum(base[slot] + word_term[pl.ds(row, 1), :], 0.0).astype(BF16)
             tiles[slot] = tile
-            partial[row] += jnp.dot(tile, band[col], preferred_element_type=F32)
+            partial[row] += jnp.dot(band[col], tile, preferred_element_type=F32)
         return carry
 
     lax.fori_loop(0, base.shape[0] // GROUP, some, 0)
 
 
-def word_products(rows, cols, base, words_all, band):
+def word_products(rows, cols, base, words_all, band, cleared):
     slots = base.shape[0]
     return pl.pallas_call(
         word_kernel,
-        in_specs=[SMEM, SMEM, VMEM, VMEM, VMEM],
+        in_specs=[SMEM, SMEM, VMEM, VMEM, VMEM, VMEM],
         out_specs=[VMEM, VMEM],
-        scratch_shapes=[pltpu.VMEM((T, ROW_TILES), F32)],
+        scratch_shapes=[pltpu.VMEM((T, ROW_TILES), F32), pltpu.VMEM((ROW_TILES, T), F32)],
         out_shape=[
             jax.ShapeDtypeStruct((slots, T, T), BF16),
             jax.ShapeDtypeStruct((ROW_TILES, T, T), F32),
         ],
+        input_output_aliases={5: 1},
         compiler_params=pltpu.CompilerParams(vmem_limit_bytes=28 << 20),
         name="word_products",
-    )(rows, cols, base, words_all, band)
+    )(rows, cols, base, words_all, band, cleared)
 
 
 AWAY = (0, 1, 0)
 
 Z_STEPS = (
-    4, (0, 0, 0), (0, 1, 1), 3, 5,
+    (0, 0, 0), (0, 1, 1), 4, 3, 5,
     (1, 1, 0), (1, 0, 1), (1, 0, 0), (1, 1, 1), (0, 0, 2), 2, 6,
     (2, 1, 0), (2, 0, 1), (2, 0, 0), (2, 1, 1), (1, 1, 2), (1, 0, 2), 1, 7,
     (3, 1, 0), (3, 0, 1), (3, 0, 0), (3, 1, 1), 0, (2, 1, 2), (2, 0, 2), None,
@@ -330,6 +340,7 @@
         trades[k].start()
 
     def term(d, lane):
+        ready(d, lane // 2)
         if lane < 2:
             return raw(d, lane, 0)
         if d not in traded:
@@ -349,9 +360,10 @@
             for lane in (0, 1):
                 for way in range(2):
                     sends[last, way, lane][1].wait_recv()
+            ready(0, 0)
             exchange(arrived(1 - y), end)
         elif isinstance(step, int):
-            ready(step)
+            ready(step, 1)
             exchange(raw(step, 1 - y, 1), step)
         else:
             s, way, lane = step
@@ -402,16 +414,22 @@
     length = NZ // 2
 
     greet([*ways, other_y, other_core])
-    swaps = {}
+    swaps, here = {}, set()
     for dz in (4, 3, 5, 2, 6, 1, 7, 0):
-        for h in range(2):
-            slot, zz = dz * 2 + h, lax.rem(z + dz, NZ)
-            swaps[dz, h] = remote(partial.at[zz, h, 1 - c], sib.at[slot], xss.at[slot], xrs.at[slot], other_core)
-            swaps[dz, h].start()
-
-    def ready(d):
-        for h in range(2):
-            swaps[d, h].wait_recv()
+        for part in range(2):
+            for h in range(2):
+                k, rows = (dz * 2 + h) * 2 + part, pl.ds(part * HALF, HALF)
+                swaps[dz, h, part] = remote(
+                    partial.at[lax.rem(z + dz, NZ), h, 1 - c, rows], sib.at[dz * 2 + h, rows],
+                    xss.at[k], xrs.at[k], other_core,
+                )
+                swaps[dz, h, part].start()
+
+    def ready(d, part):
+        if (d, part) not in here:
+            here.add((d, part))
+            for h in range(2):
+                swaps[d, h, part].wait_recv()
 
     def raw(d, h, part):
         rows = pl.ds(part * HALF, HALF)
@@ -445,15 +463,17 @@
     own = (mine.at[pair[0]], mine.at[pair[1]])
 
     def use(part, total):
+        straight = [total[t * T : (t + 1) * T].T for t in range(2)]
         for t in range(2):
-            mine[part * 2 + t] = total[t * T : (t + 1) * T].T.astype(BF16)
+            mine[part * 2 + t] = straight[t].astype(BF16)
         along_y(own[part], place(0, yh, part), 0 if part else NZ)
         for way in range(2):
             give(0, way, 2 if part else 0, own[part])
         hand(own[part], place(0, yh, part), 2 * NZ if part else 0)
         keeps.append(pltpu.make_async_copy(own[part], place(0, yh, part), ms.at[part]))
         keeps[-1].start()
-        share[pl.ds(part * HALF, HALF), :] = total
+        for t in range(2):
+            share[pl.ds(part * HALF + t * T, T), :] = straight[t]
 
     drain = ring_sum(Z_STEPS, length, yh, raw, ready, ways, other_y, use, *ring)
     passes[NZ].wait_recv()
@@ -505,7 +525,7 @@
         scratch_shapes=[
             pltpu.VMEM((2 * NZ, SHARE, T), F32),
             pltpu.VMEM((4, T, T), BF16),
-            DMA((2 * NZ,)), DMA((2 * NZ,)), DMA((3 * NZ,)), DMA((3 * NZ,)),
+            DMA((4 * NZ,)), DMA((4 * NZ,)), DMA((3 * NZ,)), DMA((3 * NZ,)),
             DMA((4 * NZ,)), DMA((4 * NZ,)), DMA((NZ + 1,)), DMA((NZ + 1,)), DMA((2,)),
             *ring_scratch(Z_STEPS, NZ // 2),
         ],
@@ -514,20 +534,17 @@
     )(partial)
 
 
-def context_kernel(rows, cols, tiles, rounded, share, partial, share_out, odd):
+def context_kernel(rows, cols, tiles, rounded, share, partial, share_out):
     share_out[...] = share[...]
-    sums = (partial, odd)
-    for ref in sums:
-        ref[...] = jnp.zeros_like(ref)
+    partial[...] = jnp.zeros_like(partial)
 
     def some(b, carry):
         for g in range(GROUP):
             slot = b * GROUP + g
-            sums[g % 2][cols[slot]] += jnp.dot(rounded[rows[slot]], tiles[slot], preferred_element_type=F32)
+            partial[cols[slot]] += jnp.dot(tiles[slot], rounded[rows[slot]], preferred_element_type=F32)
         return carry
 
     lax.fori_loop(0, tiles.shape[0] // GROUP, some, 0)
-    partial[...] += odd[...]
 
 
 def context_products(rows, cols, tiles, rounded, share):
@@ -540,7 +557,6 @@
             jax.ShapeDtypeStruct((COL_TILES, T, T), F32),
             jax.ShapeDtypeStruct((SHARE, T), F32),
         ],
-        scratch_shapes=[pltpu.VMEM((COL_TILES, T, T), F32)],
         compiler_params=pltpu.CompilerParams(vmem_limit_bytes=16 << 20),
         name="context_products",
     )(rows, cols, tiles, rounded, share)
@@ -556,11 +572,9 @@
         return partial[h, lax.rem(x + d, NX), pl.ds(part * HALF, HALF), :]
 
     def use(part, total):
-        total = total * (1.0 / T)
-        for t in range(2):
-            share[pl.ds(part * HALF + t * T, T), :] = total[t * T : (t + 1) * T].T
-
-    ring_sum(X_STEPS, NX // 2, yl, raw, lambda d: None, ways, other_y, use, *ring)()
+        share[pl.ds(part * HALF, HALF), :] = total * (1.0 / T)
+
+    ring_sum(X_STEPS, NX // 2, yl, raw, lambda d, part: None, ways, other_y, use, *ring)()
 
 
 def context_panel_sum(partial):
@@ -578,9 +592,9 @@
 def shards(tile_counts, tile_rows, tile_cols, panel):
     counts, rows, cols = tile_counts[0, 0], tile_rows[0, 0], tile_cols[0, 0]
     far = [pltpu.with_memory_space_constraint(a, pltpu.HBM) for a in (rows, cols, counts, panel)]
-    words_all, band, base = totals(*far)
+    words_all, band, base, cleared = totals(*far)
     band = band.reshape(COL_TILES, T, T)
-    tiles, partial = word_products(rows, cols, base, words_all, band)
+    tiles, partial = word_products(rows, cols, base, words_all, band, cleared)
     share, everyone = word_panel_sum(partial.reshape(NZ, NYH, NC, SHARE, T))
     rounded = everyone.reshape(ROW_TILES, T, T)
     context_partial, share = context_products(rows, cols, tiles, rounded, share)

time: 104 us -> 105 us (level)
    pallas_call x1, Pallas kernels: 6.87 us -> 3.78 us  [word_products(): pl.pallas_call(word_kernel, in_specs=[SMEM, SMEM, VMEM, VMEM, VMEM, VMEM]...]
    pallas_call x1, Pallas kernels: 26.8 us -> 29.5 us  [totals(): pl.pallas_call(totals_kernel, in_specs=[ANY, ANY, ANY, ANY], out_specs=[V...]
    pallas_call x1, Pallas kernels: 49.3 us -> 51.1 us  [word_panel_sum(): pl.pallas_call(word_panel_kernel, in_specs=[VMEM], out_specs=[VMEM, ANY],...]
where the time goes in v6:
time: 105 us
  Pallas kernels  104 us (99%)
    pallas_call x1, Pallas kernels, word_panel_sum(): pl.pallas_call(word_panel_kernel, in_specs=[VMEM], out_specs=[VMEM, ANY],...  51.1 us
    pallas_call x1, Pallas kernels, totals(): pl.pallas_call(totals_kernel, in_specs=[ANY, ANY, ANY, ANY], out_specs=[V...  29.5 us
    pallas_call x1, Pallas kernels, context_panel_sum(): pl.pallas_call(context_panel_kernel, in_specs=[VMEM], out_specs=VMEM, out...  14.9 us
    pallas_call x1, Pallas kernels, context_products(): pl.pallas_call(context_kernel, in_specs=[SMEM, SMEM, VMEM, VMEM, VMEM], o...  4.49 us
    pallas_call x1, Pallas kernels, word_products(): pl.pallas_call(word_kernel, in_specs=[SMEM, SMEM, VMEM, VMEM, VMEM, VMEM]...  3.78 us

profile of v6, /device:TPU:8, one launch (start us, length us, event | category | flops | bytes accessed | tf_op | source)
XLA Modules:
  0.0 105.2 jit_solution(8324253509144201224)
XLA Ops:
  0.6 0.0 copy-start.1
  0.6 0.0 copy-start
  0.7 29.5 %totals.1 = (f32[8,24,128]{2,1,0:T(8,128)S(1)}, bf16[8,512,128]{2,1,0:T(8,128)(2,1)S(1)}, f32[160,128,128]{2,1,0:T(8,128)S(1)}, f32[128,128,128]{2,1,0:T(8,128)S(1)}) custom-call(s32[160]{0:T(256)} %bitcast.11, s32[160]{0:T(256)} %bitcast.14, s32[160,128,128]{2,1,0:T(8,128)} %bitcast.17, bf16[512,128]{1,0:T(8,128)(2,1)} %panel_in.1), custom_call_target="tpu_custom_call" | custom-call | tf_op jit(solution)/shard_map/totals/pallas_call | solution.py:247
  30.2 0.0 copy-done.1
  30.2 0.0 copy-done
  30.2 3.8 %word_products.1 = (bf16[160,128,128]{2,1,0:T(8,128)(2,1)S(1)}, f32[128,128,128]{2,1,0:T(8,128)S(1)}) custom-call(s32[160]{0:T(256)S(1)} %bitcast.12, s32[160]{0:T(256)S(1)} %bitcast.15, f32[160,128,128]{2,1,0:T(8,128)S(1)} %get-tuple-element.12.base, f32[8,24,128]{2,1,0:T(8,128)S(1)} %get-tuple-element.13.words_all, ...), custom_call_target="tpu_custom_call", output_to_operand_aliasing={{1}: (5, {})} | custom-call | tf_op jit(solution)/shard_map/word_products/pallas_call | solution.py:301
  34.0 51.1 %word_panel_sum.1 = (f32[512,128]{1,0:T(8,128)S(1)}, bf16[8,2,2,4,128,128]{5,4,3,2,1,0:T(8,128)(2,1)S(1)}) custom-call(f32[8,2,2,512,128]{4,3,2,1,0:T(8,128)S(1)} %bitcast.7), custom_call_target="tpu_custom_call" | custom-call | tf_op jit(solution)/shard_map/word_panel_sum/pallas_call | solution.py:517
  85.0 4.5 %context_products.1 = (f32[32,128,128]{2,1,0:T(8,128)S(1)}, f32[512,128]{1,0:T(8,128)}) custom-call(s32[160]{0:T(256)S(1)} %bitcast.13, s32[160]{0:T(256)S(1)} %bitcast.16, bf16[160,128,128]{2,1,0:T(8,128)(2,1)S(1)} %get-tuple-element.16.tiles, bf16[128,128,128]{2,1,0:T(8,128)(2,1)S(1)} %bitcast.8, f32[512,128]{1,0:T(8,128)S(1)} %get-tuple-element.19.share), custom_call_target="tpu_custom_call" | custom-call | tf_op jit(solution)/shard_map/context_products/pallas_call | solution.py:552
  89.5 14.9 %context_panel_sum.1 = f32[512,128]{1,0:T(8,128)S(1)} custom-call(f32[2,4,512,128]{3,2,1,0:T(8,128)S(1)} %bitcast.9), custom_call_target="tpu_custom_call" | custom-call | tf_op jit(solution)/shard_map/context_panel_sum/pallas_call | solution.py:581
  104.5 0.7 copy.9
Async XLA Ops:
  0.6 29.5 %copy-start.1 = (s32[1,1,160]{2,1,0:T(1,128)S(1)}, s32[1,1,160]{2,1,0:T(1,128)}, u32[]{:S(2)}) copy-start(s32[1,1,160]{2,1,0:T(1,128)} %param.6) | copy-start | bytes 1924
  0.6 29.5 %copy-start = (s32[1,1,160]{2,1,0:T(1,128)S(1)}, s32[1,1,160]{2,1,0:T(1,128)}, u32[]{:S(2)}) copy-start(s32[1,1,160]{2,1,0:T(1,128)} %param.5) | copy-start | bytes 1924

commit v7 on v6

--- a/solution.py
+++ b/solution.py
@@ -108,10 +108,9 @@
         pltpu.make_async_copy(cols_in, cols, lsem.at[2]),
     ]
     bring = pltpu.make_async_copy(panel_in, brought, lsem.at[3])
-    for copy in slots:
+    for copy in (bring, *slots):
         copy.start()
     load_counts(counts, held, cs)
-    bring.start()
     hail(everybody)
     bring.wait()
     for t in range(4):
@@ -476,14 +475,15 @@
             share[pl.ds(part * HALF + t * T, T), :] = straight[t]
 
     drain = ring_sum(Z_STEPS, length, yh, raw, ready, ways, other_y, use, *ring)
-    passes[NZ].wait_recv()
-    for way in range(2):
-        give(0, way, 1)
-    hand(lane_place(0, 1), lane_place(0, 1), 1)
     due = [0]
     for s in range(1, length + 1):
         came = []
         for lane in (0, 2, 1) if s == 1 else (2, 0, 1):
+            if s == 1 and lane == 1:
+                passes[NZ].wait_recv()
+                for way in range(2):
+                    give(0, way, 1)
+                hand(lane_place(0, 1), lane_place(0, 1), 1)
             for way in range(2):
                 if (s - 1, way, lane) not in gives:
                     continue

time: 105 us -> 104 us (level)
  no operation moved by 1% of the time
where the time goes in v7:
time: 104 us
  Pallas kernels  103 us (99%)
    pallas_call x1, Pallas kernels, word_panel_sum(): pl.pallas_call(word_panel_kernel, in_specs=[VMEM], out_specs=[VMEM, ANY],...  50.9 us
    pallas_call x1, Pallas kernels, totals(): pl.pallas_call(totals_kernel, in_specs=[ANY, ANY, ANY, ANY], out_specs=[V...  28.6 us
    pallas_call x1, Pallas kernels, context_panel_sum(): pl.pallas_call(context_panel_kernel, in_specs=[VMEM], out_specs=VMEM, out...  14.9 us
    pallas_call x1, Pallas kernels, context_products(): pl.pallas_call(context_kernel, in_specs=[SMEM, SMEM, VMEM, VMEM, VMEM], o...  4.49 us
    pallas_call x1, Pallas kernels, word_products(): pl.pallas_call(word_kernel, in_specs=[SMEM, SMEM, VMEM, VMEM, VMEM, VMEM]...  3.77 us

profile of v7, /device:TPU:8, one launch (start us, length us, event | category | flops | bytes accessed | tf_op | source)
XLA Modules:
  0.0 104.1 jit_solution(2893416656003965347)
XLA Ops:
  0.6 0.0 copy-start.1
  0.6 0.0 copy-start
  0.7 28.6 %totals.1 = (f32[8,24,128]{2,1,0:T(8,128)S(1)}, bf16[8,512,128]{2,1,0:T(8,128)(2,1)S(1)}, f32[160,128,128]{2,1,0:T(8,128)S(1)}, f32[128,128,128]{2,1,0:T(8,128)S(1)}) custom-call(s32[160]{0:T(256)} %bitcast.11, s32[160]{0:T(256)} %bitcast.14, s32[160,128,128]{2,1,0:T(8,128)} %bitcast.17, bf16[512,128]{1,0:T(8,128)(2,1)} %panel_in.1), custom_call_target="tpu_custom_call" | custom-call | tf_op jit(solution)/shard_map/totals/pallas_call | solution.py:246
  29.3 0.0 copy-done.1
  29.3 0.0 copy-done
  29.3 3.8 %word_products.1 = (bf16[160,128,128]{2,1,0:T(8,128)(2,1)S(1)}, f32[128,128,128]{2,1,0:T(8,128)S(1)}) custom-call(s32[160]{0:T(256)S(1)} %bitcast.12, s32[160]{0:T(256)S(1)} %bitcast.15, f32[160,128,128]{2,1,0:T(8,128)S(1)} %get-tuple-element.12.base, f32[8,24,128]{2,1,0:T(8,128)S(1)} %get-tuple-element.13.words_all, ...), custom_call_target="tpu_custom_call", output_to_operand_aliasing={{1}: (5, {})} | custom-call | tf_op jit(solution)/shard_map/word_products/pallas_call | solution.py:300
  33.1 50.9 %word_panel_sum.1 = (f32[512,128]{1,0:T(8,128)S(1)}, bf16[8,2,2,4,128,128]{5,4,3,2,1,0:T(8,128)(2,1)S(1)}) custom-call(f32[8,2,2,512,128]{4,3,2,1,0:T(8,128)S(1)} %bitcast.7), custom_call_target="tpu_custom_call" | custom-call | tf_op jit(solution)/shard_map/word_panel_sum/pallas_call | solution.py:517
  84.0 4.5 %context_products.1 = (f32[32,128,128]{2,1,0:T(8,128)S(1)}, f32[512,128]{1,0:T(8,128)}) custom-call(s32[160]{0:T(256)S(1)} %bitcast.13, s32[160]{0:T(256)S(1)} %bitcast.16, bf16[160,128,128]{2,1,0:T(8,128)(2,1)S(1)} %get-tuple-element.16.tiles, bf16[128,128,128]{2,1,0:T(8,128)(2,1)S(1)} %bitcast.8, f32[512,128]{1,0:T(8,128)S(1)} %get-tuple-element.19.share), custom_call_target="tpu_custom_call" | custom-call | tf_op jit(solution)/shard_map/context_products/pallas_call | solution.py:552
  88.5 14.9 %context_panel_sum.1 = f32[512,128]{1,0:T(8,128)S(1)} custom-call(f32[2,4,512,128]{3,2,1,0:T(8,128)S(1)} %bitcast.9), custom_call_target="tpu_custom_call" | custom-call | tf_op jit(solution)/shard_map/context_panel_sum/pallas_call | solution.py:581
  103.4 0.7 copy.9
Async XLA Ops:
  0.6 28.6 %copy-start.1 = (s32[1,1,160]{2,1,0:T(1,128)S(1)}, s32[1,1,160]{2,1,0:T(1,128)}, u32[]{:S(2)}) copy-start(s32[1,1,160]{2,1,0:T(1,128)} %param.6) | copy-start | bytes 1924
  0.6 28.6 %copy-start = (s32[1,1,160]{2,1,0:T(1,128)S(1)}, s32[1,1,160]{2,1,0:T(1,128)}, u32[]{:S(2)}) copy-start(s32[1,1,160]{2,1,0:T(1,128)} %param.5) | copy-start | bytes 1924

commit v8 on v6

--- a/solution.py
+++ b/solution.py
@@ -108,11 +108,10 @@
         pltpu.make_async_copy(cols_in, cols, lsem.at[2]),
     ]
     bring = pltpu.make_async_copy(panel_in, brought, lsem.at[3])
-    for copy in slots:
+    hail(everybody)
+    for copy in (bring, *slots):
         copy.start()
     load_counts(counts, held, cs)
-    bring.start()
-    hail(everybody)
     bring.wait()
     for t in range(4):
         tile = pl.ds(t * T, T)
@@ -123,6 +122,7 @@
     wacc[...] = jnp.zeros_like(wacc)
     lanes = lax.broadcasted_iota(I32, (T, T), 1)
     bands = lax.broadcasted_iota(I32, (COL_TILES, T), 0)
+    ones = jnp.ones((2 * T, T), BF16)
     for copy in slots:
         copy.wait()
 
@@ -135,7 +135,12 @@
             per_context = per_context + jnp.where(
                 bands == cols[slot], jnp.sum(value, axis=0, keepdims=True), 0
             )
-            sums = jnp.sum(value.astype(F32), axis=1, keepdims=True)
+            if g % 4 == 3:
+                eights = jnp.bitwise_and(value, -8)
+                parts = [a.astype(F32).astype(BF16) for a in (eights, value - eights)]
+                sums = jnp.dot(jnp.concatenate(parts, axis=1), ones, preferred_element_type=F32)
+            else:
+                sums = jnp.sum(value.astype(F32), axis=1, keepdims=True)
             per_word = per_word + jnp.where(lanes == rows[slot], sums, 0.0)
         wacc[...] = per_word
         return per_context

time: 105 us -> 104 us (level)
  no operation moved by 1% of the time
where the time goes in v8:
time: 104 us
  Pallas kernels  103 us (99%)
    pallas_call x1, Pallas kernels, word_panel_sum(): pl.pallas_call(word_panel_kernel, in_specs=[VMEM], out_specs=[VMEM, ANY],...  51.1 us
    pallas_call x1, Pallas kernels, totals(): pl.pallas_call(totals_kernel, in_specs=[ANY, ANY, ANY, ANY], out_specs=[V...  28.8 us
    pallas_call x1, Pallas kernels, context_panel_sum(): pl.pallas_call(context_panel_kernel, in_specs=[VMEM], out_specs=VMEM, out...  14.9 us
    pallas_call x1, Pallas kernels, context_products(): pl.pallas_call(context_kernel, in_specs=[SMEM, SMEM, VMEM, VMEM, VMEM], o...  4.42 us
    pallas_call x1, Pallas kernels, word_products(): pl.pallas_call(word_kernel, in_specs=[SMEM, SMEM, VMEM, VMEM, VMEM, VMEM]...  3.77 us

profile of v8, /device:TPU:8, one launch (start us, length us, event | category | flops | bytes accessed | tf_op | source)
XLA Modules:
  0.0 104.4 jit_solution(6694150471355294694)
XLA Ops:
  0.6 0.0 copy-start.1
  0.6 0.0 copy-start
  0.7 28.8 %totals.1 = (f32[8,24,128]{2,1,0:T(8,128)S(1)}, bf16[8,512,128]{2,1,0:T(8,128)(2,1)S(1)}, f32[160,128,128]{2,1,0:T(8,128)S(1)}, f32[128,128,128]{2,1,0:T(8,128)S(1)}) custom-call(s32[160]{0:T(256)} %bitcast.11, s32[160]{0:T(256)} %bitcast.14, s32[160,128,128]{2,1,0:T(8,128)} %bitcast.17, bf16[512,128]{1,0:T(8,128)(2,1)} %panel_in.1), custom_call_target="tpu_custom_call" | custom-call | tf_op jit(solution)/shard_map/totals/pallas_call | solution.py:252
  29.5 0.0 copy-done.1
  29.5 0.0 copy-done
  29.5 3.8 %word_products.1 = (bf16[160,128,128]{2,1,0:T(8,128)(2,1)S(1)}, f32[128,128,128]{2,1,0:T(8,128)S(1)}) custom-call(s32[160]{0:T(256)S(1)} %bitcast.12, s32[160]{0:T(256)S(1)} %bitcast.15, f32[160,128,128]{2,1,0:T(8,128)S(1)} %get-tuple-element.12.base, f32[8,24,128]{2,1,0:T(8,128)S(1)} %get-tuple-element.13.words_all, ...), custom_call_target="tpu_custom_call", output_to_operand_aliasing={{1}: (5, {})} | custom-call | tf_op jit(solution)/shard_map/word_products/pallas_call | solution.py:306
  33.3 51.1 %word_panel_sum.1 = (f32[512,128]{1,0:T(8,128)S(1)}, bf16[8,2,2,4,128,128]{5,4,3,2,1,0:T(8,128)(2,1)S(1)}) custom-call(f32[8,2,2,512,128]{4,3,2,1,0:T(8,128)S(1)} %bitcast.7), custom_call_target="tpu_custom_call" | custom-call | tf_op jit(solution)/shard_map/word_panel_sum/pallas_call | solution.py:522
  84.3 4.4 %context_products.1 = (f32[32,128,128]{2,1,0:T(8,128)S(1)}, f32[512,128]{1,0:T(8,128)}) custom-call(s32[160]{0:T(256)S(1)} %bitcast.13, s32[160]{0:T(256)S(1)} %bitcast.16, bf16[160,128,128]{2,1,0:T(8,128)(2,1)S(1)} %get-tuple-element.16.tiles, bf16[128,128,128]{2,1,0:T(8,128)(2,1)S(1)} %bitcast.8, f32[512,128]{1,0:T(8,128)S(1)} %get-tuple-element.19.share), custom_call_target="tpu_custom_call" | custom-call | tf_op jit(solution)/shard_map/context_products/pallas_call | solution.py:557
  88.8 14.9 %context_panel_sum.1 = f32[512,128]{1,0:T(8,128)S(1)} custom-call(f32[2,4,512,128]{3,2,1,0:T(8,128)S(1)} %bitcast.9), custom_call_target="tpu_custom_call" | custom-call | tf_op jit(solution)/shard_map/context_panel_sum/pallas_call | solution.py:586
  103.7 0.7 copy.9
Async XLA Ops:
  0.6 28.8 %copy-start.1 = (s32[1,1,160]{2,1,0:T(1,128)S(1)}, s32[1,1,160]{2,1,0:T(1,128)}, u32[]{:S(2)}) copy-start(s32[1,1,160]{2,1,0:T(1,128)} %param.6) | copy-start | bytes 1924
  0.6 28.8 %copy-start = (s32[1,1,160]{2,1,0:T(1,128)S(1)}, s32[1,1,160]{2,1,0:T(1,128)}, u32[]{:S(2)}) copy-start(s32[1,1,160]{2,1,0:T(1,128)} %param.5) | copy-start | bytes 1924

commit v9 on v8

--- a/solution.py
+++ b/solution.py
@@ -112,12 +112,6 @@
     for copy in (bring, *slots):
         copy.start()
     load_counts(counts, held, cs)
-    bring.wait()
-    for t in range(4):
-        tile = pl.ds(t * T, T)
-        panel[tile, :] = brought[tile, :].astype(F32).T.astype(BF16)
-    own = pltpu.make_async_copy(panel, band.at[row], lsem.at[0])
-    own.start()
 
     wacc[...] = jnp.zeros_like(wacc)
     lanes = lax.broadcasted_iota(I32, (T, T), 1)
@@ -159,6 +153,13 @@
     for copy in wsends:
         copy.start()
 
+    bring.wait()
+    for t in range(4):
+        tile = pl.ds(t * T, T)
+        panel[tile, :] = brought[tile, :].astype(F32).T.astype(BF16)
+    own = pltpu.make_async_copy(panel, band.at[row], lsem.at[0])
+    own.start()
+
     psends = []
 
     def pass_on(src, dst, device):
@@ -192,12 +193,6 @@
     powers = powers_of(contexts_sum)
     band_power = jnp.sum(powers, keepdims=True)
     context_log[...] = jnp.log(jnp.maximum(powers, 1.0))
-
-    for copy in psends[0:3]:
-        copy.wait_recv()
-    there = band.at[(1 - yl) * NX + x]
-    to_right_and_left(there, there)
-    relay(yl)
 
     for copy in wsends:
         copy.wait_recv()
@@ -219,6 +214,12 @@
             )
             base[slot] = term.T
         return carry
+
+    for copy in psends[0:3]:
+        copy.wait_recv()
+    there = band.at[(1 - yl) * NX + x]
+    to_right_and_left(there, there)
+    relay(yl)
 
     lax.fori_loop(0, blocks // 2, logs, 0)
     for copy in qsends:
@@ -233,10 +234,10 @@
     for copy in asends:
         copy.start()
 
-    lax.fori_loop(blocks // 2, blocks, logs, 0)
     for copy in psends[3:5]:
         copy.wait_recv()
     relay(1 - yl)
+    lax.fori_loop(blocks // 2, blocks, logs, 0)
 
     for copy in asends:
         copy.wait()

time: 104 us -> 102 us (0.981)
  Pallas kernels: 103 us -> 100 us
    pallas_call x1, Pallas kernels: 28.8 us -> 25.1 us  [totals(): pl.pallas_call(totals_kernel, in_specs=[ANY, ANY, ANY, ANY], out_specs=[V...]
    pallas_call x1, Pallas kernels: 51.1 us -> 52.3 us  [word_panel_sum(): pl.pallas_call(word_panel_kernel, in_specs=[VMEM], out_specs=[VMEM, ANY],...]
where the time goes in v9:
time: 102 us
  Pallas kernels  100 us (98%)
    pallas_call x1, Pallas kernels, word_panel_sum(): pl.pallas_call(word_panel_kernel, in_specs=[VMEM], out_specs=[VMEM, ANY],...  52.3 us
    pallas_call x1, Pallas kernels, totals(): pl.pallas_call(totals_kernel, in_specs=[ANY, ANY, ANY, ANY], out_specs=[V...  25.1 us
    pallas_call x1, Pallas kernels, context_panel_sum(): pl.pallas_call(context_panel_kernel, in_specs=[VMEM], out_specs=VMEM, out...  14.9 us
    pallas_call x1, Pallas kernels, context_products(): pl.pallas_call(context_kernel, in_specs=[SMEM, SMEM, VMEM, VMEM, VMEM], o...  4.44 us
    pallas_call x1, Pallas kernels, word_products(): pl.pallas_call(word_kernel, in_specs=[SMEM, SMEM, VMEM, VMEM, VMEM, VMEM]...  3.76 us

profile of v9, /device:TPU:8, one launch (start us, length us, event | category | flops | bytes accessed | tf_op | source)
XLA Modules:
  0.0 101.9 jit_solution(16148526442954632878)
XLA Ops:
  0.6 0.0 copy-start.1
  0.6 0.0 copy-start
  0.7 25.1 %totals.1 = (f32[8,24,128]{2,1,0:T(8,128)S(1)}, bf16[8,512,128]{2,1,0:T(8,128)(2,1)S(1)}, f32[160,128,128]{2,1,0:T(8,128)S(1)}, f32[128,128,128]{2,1,0:T(8,128)S(1)}) custom-call(s32[160]{0:T(256)} %bitcast.11, s32[160]{0:T(256)} %bitcast.14, s32[160,128,128]{2,1,0:T(8,128)} %bitcast.17, bf16[512,128]{1,0:T(8,128)(2,1)} %panel_in.1), custom_call_target="tpu_custom_call" | custom-call | tf_op jit(solution)/shard_map/totals/pallas_call | solution.py:253
  25.7 0.0 copy-done.1
  25.8 0.0 copy-done
  25.8 3.8 %word_products.1 = (bf16[160,128,128]{2,1,0:T(8,128)(2,1)S(1)}, f32[128,128,128]{2,1,0:T(8,128)S(1)}) custom-call(s32[160]{0:T(256)S(1)} %bitcast.12, s32[160]{0:T(256)S(1)} %bitcast.15, f32[160,128,128]{2,1,0:T(8,128)S(1)} %get-tuple-element.12.base, f32[8,24,128]{2,1,0:T(8,128)S(1)} %get-tuple-element.13.words_all, ...), custom_call_target="tpu_custom_call", output_to_operand_aliasing={{1}: (5, {})} | custom-call | tf_op jit(solution)/shard_map/word_products/pallas_call | solution.py:307
  29.5 52.3 %word_panel_sum.1 = (f32[512,128]{1,0:T(8,128)S(1)}, bf16[8,2,2,4,128,128]{5,4,3,2,1,0:T(8,128)(2,1)S(1)}) custom-call(f32[8,2,2,512,128]{4,3,2,1,0:T(8,128)S(1)} %bitcast.7), custom_call_target="tpu_custom_call" | custom-call | tf_op jit(solution)/shard_map/word_panel_sum/pallas_call | solution.py:523
  81.8 4.4 %context_products.1 = (f32[32,128,128]{2,1,0:T(8,128)S(1)}, f32[512,128]{1,0:T(8,128)}) custom-call(s32[160]{0:T(256)S(1)} %bitcast.13, s32[160]{0:T(256)S(1)} %bitcast.16, bf16[160,128,128]{2,1,0:T(8,128)(2,1)S(1)} %get-tuple-element.16.tiles, bf16[128,128,128]{2,1,0:T(8,128)(2,1)S(1)} %bitcast.8, f32[512,128]{1,0:T(8,128)S(1)} %get-tuple-element.19.share), custom_call_target="tpu_custom_call" | custom-call | tf_op jit(solution)/shard_map/context_products/pallas_call | solution.py:558
  86.3 14.9 %context_panel_sum.1 = f32[512,128]{1,0:T(8,128)S(1)} custom-call(f32[2,4,512,128]{3,2,1,0:T(8,128)S(1)} %bitcast.9), custom_call_target="tpu_custom_call" | custom-call | tf_op jit(solution)/shard_map/context_panel_sum/pallas_call | solution.py:587
  101.2 0.7 copy.9
Async XLA Ops:
  0.6 25.1 %copy-start.1 = (s32[1,1,160]{2,1,0:T(1,128)S(1)}, s32[1,1,160]{2,1,0:T(1,128)}, u32[]{:S(2)}) copy-start(s32[1,1,160]{2,1,0:T(1,128)} %param.6) | copy-start | bytes 1924
  0.6 25.1 %copy-start = (s32[1,1,160]{2,1,0:T(1,128)S(1)}, s32[1,1,160]{2,1,0:T(1,128)}, u32[]{:S(2)}) copy-start(s32[1,1,160]{2,1,0:T(1,128)} %param.5) | copy-start | bytes 1924

commit v10 on v9

--- a/solution.py
+++ b/solution.py
@@ -321,6 +321,8 @@
 
 AWAY = (0, 1, 0)
 
+ACROSS = (0, 2, 2)
+
 Z_STEPS = (
     (0, 0, 0), (0, 1, 1), 4, 3, 5,
     (1, 1, 0), (1, 0, 1), (1, 0, 0), (1, 1, 1), (0, 0, 2), 2, 6,
@@ -330,8 +332,8 @@
 )
 X_STEPS = (
     2, (0, 0, 0), (0, 1, 1), 1, 3,
-    (1, 1, 0), (1, 0, 1), (0, 0, 2), (1, 0, 0), (1, 1, 1), 0, None,
-    (1, 1, 2), (1, 0, 2),
+    (1, 1, 0), (1, 0, 1), (1, 0, 0), (1, 1, 1), ACROSS, 0,
+    (1, 0, 2), (1, 1, 2), None,
 )
 
 
@@ -373,7 +375,7 @@
             exchange(raw(step, 1 - y, 1), step)
         else:
             s, way, lane = step
-            value = term(length - s if way == 0 else length + s, lane)
+            value = term(length + s if way == 1 else length - s, lane)
             if (s - 1, way, lane) in sends:
                 index, before = sends[s - 1, way, lane]
                 before.wait_recv()
@@ -388,10 +390,11 @@
     trades[end].wait_recv()
     use(0, first + decode(yrecvb.at[end]))
     second = term(0, 2)
-    for way in range(2):
-        index, copy = sends[last, way, 2]
-        copy.wait_recv()
-        second = second + decode(recvb.at[index])
+    for step in ((last, 0, 2), (last, 1, 2), ACROSS):
+        if step in sends:
+            index, copy = sends[step]
+            copy.wait_recv()
+            second = second + decode(recvb.at[index])
     use(1, second)
 
     def drain():
@@ -412,7 +415,7 @@
     ]
 
 
-def word_panel_kernel(partial, share, everyone, sib, mine, xss, xrs, gss, grs, hss, hrs, pss, prs, ms,
+def word_panel_kernel(partial, share, everyone, cleared, sib, mine, xss, xrs, gss, grs, hss, hrs, pss, prs, ms,
                       *ring):
     z, yh, c = lax.axis_index("z"), lax.axis_index("yh"), lax.axis_index("core")
     ways = ({"z": lax.rem(z + 1, NZ)}, {"z": lax.rem(z + NZ - 1, NZ)})
@@ -430,6 +433,12 @@
                     xss.at[k], xrs.at[k], other_core,
                 )
                 swaps[dz, h, part].start()
+
+    def clear(t, carry):
+        cleared[t] = jnp.zeros((T, T), F32)
+        return carry
+
+    lax.fori_loop(0, COL_TILES, clear, 0)
 
     def ready(d, part):
         if (d, part) not in here:
@@ -523,10 +532,11 @@
     return pl.pallas_call(
         word_panel_kernel,
         in_specs=[VMEM],
-        out_specs=[VMEM, ANY],
+        out_specs=[VMEM, ANY, VMEM],
         out_shape=[
             jax.ShapeDtypeStruct((SHARE, T), F32),
             jax.ShapeDtypeStruct((NZ, NYH, NC, 4, T, T), BF16),
+            jax.ShapeDtypeStruct((COL_TILES, T, T), F32),
         ],
         scratch_shapes=[
             pltpu.VMEM((2 * NZ, SHARE, T), F32),
@@ -540,9 +550,8 @@
     )(partial)
 
 
-def context_kernel(rows, cols, tiles, rounded, share, partial, share_out):
+def context_kernel(rows, cols, tiles, rounded, share, cleared, partial, share_out):
     share_out[...] = share[...]
-    partial[...] = jnp.zeros_like(partial)
 
     def some(b, carry):
         for g in range(GROUP):
@@ -553,24 +562,25 @@
     lax.fori_loop(0, tiles.shape[0] // GROUP, some, 0)
 
 
-def context_products(rows, cols, tiles, rounded, share):
+def context_products(rows, cols, tiles, rounded, share, cleared):
     slots = tiles.shape[0]
     return pl.pallas_call(
         context_kernel,
-        in_specs=[SMEM, SMEM, VMEM, VMEM, VMEM],
+        in_specs=[SMEM, SMEM, VMEM, VMEM, VMEM, VMEM],
         out_specs=[VMEM, VMEM],
+        input_output_aliases={5: 0},
         out_shape=[
             jax.ShapeDtypeStruct((COL_TILES, T, T), F32),
             jax.ShapeDtypeStruct((SHARE, T), F32),
         ],
         compiler_params=pltpu.CompilerParams(vmem_limit_bytes=16 << 20),
         name="context_products",
-    )(rows, cols, tiles, rounded, share)
+    )(rows, cols, tiles, rounded, share, cleared)
 
 
 def context_panel_kernel(partial, share, *ring):
     x, yl = lax.axis_index("x"), lax.axis_index("yl")
-    ways = ({"x": lax.rem(x + 1, NX)}, {"x": lax.rem(x + NX - 1, NX)})
+    ways = tuple({"x": lax.rem(x + d, NX)} for d in (1, NX - 1, NX // 2))
     other_y = {"yl": 1 - yl}
     greet([*ways, other_y])
 
@@ -601,9 +611,9 @@
     words_all, band, base, cleared = totals(*far)
     band = band.reshape(COL_TILES, T, T)
     tiles, partial = word_products(rows, cols, base, words_all, band, cleared)
-    share, everyone = word_panel_sum(partial.reshape(NZ, NYH, NC, SHARE, T))
+    share, everyone, clear_contexts = word_panel_sum(partial.reshape(NZ, NYH, NC, SHARE, T))
     rounded = everyone.reshape(ROW_TILES, T, T)
-    context_partial, share = context_products(rows, cols, tiles, rounded, share)
+    context_partial, share = context_products(rows, cols, tiles, rounded, share, clear_contexts)
     context_share = context_panel_sum(context_partial.reshape(NYL, NX, SHARE, T))
     return share, context_share
 

time: 102 us -> 102 us (level)
  no operation moved by 1% of the time
where the time goes in v10:
time: 102 us
  Pallas kernels  100 us (98%)
    pallas_call x1, Pallas kernels, word_panel_sum(): pl.pallas_call(word_panel_kernel, in_specs=[VMEM], out_specs=[VMEM, ANY,...  52.4 us
    pallas_call x1, Pallas kernels, totals(): pl.pallas_call(totals_kernel, in_specs=[ANY, ANY, ANY, ANY], out_specs=[V...  25.1 us
    pallas_call x1, Pallas kernels, context_panel_sum(): pl.pallas_call(context_panel_kernel, in_specs=[VMEM], out_specs=VMEM, out...  14.6 us
    pallas_call x1, Pallas kernels, context_products(): pl.pallas_call(context_kernel, in_specs=[SMEM, SMEM, VMEM, VMEM, VMEM, VM...  4.45 us
    pallas_call x1, Pallas kernels, word_products(): pl.pallas_call(word_kernel, in_specs=[SMEM, SMEM, VMEM, VMEM, VMEM, VMEM]...  3.79 us

profile of v10, /device:TPU:8, one launch (start us, length us, event | category | flops | bytes accessed | tf_op | source)
XLA Modules:
  0.0 101.7 jit_solution(8949659136017056639)
XLA Ops:
  0.6 0.0 copy-start.1
  0.6 0.0 copy-start
  0.7 25.1 %totals.1 = (f32[8,24,128]{2,1,0:T(8,128)S(1)}, bf16[8,512,128]{2,1,0:T(8,128)(2,1)S(1)}, f32[160,128,128]{2,1,0:T(8,128)S(1)}, f32[128,128,128]{2,1,0:T(8,128)S(1)}) custom-call(s32[160]{0:T(256)} %bitcast.11, s32[160]{0:T(256)} %bitcast.14, s32[160,128,128]{2,1,0:T(8,128)} %bitcast.17, bf16[512,128]{1,0:T(8,128)(2,1)} %panel_in.1), custom_call_target="tpu_custom_call" | custom-call | tf_op jit(solution)/shard_map/totals/pallas_call | solution.py:253
  25.7 0.0 copy-done.1
  25.8 0.0 copy-done
  25.8 3.8 %word_products.1 = (bf16[160,128,128]{2,1,0:T(8,128)(2,1)S(1)}, f32[128,128,128]{2,1,0:T(8,128)S(1)}) custom-call(s32[160]{0:T(256)S(1)} %bitcast.12, s32[160]{0:T(256)S(1)} %bitcast.15, f32[160,128,128]{2,1,0:T(8,128)S(1)} %get-tuple-element.13.base, f32[8,24,128]{2,1,0:T(8,128)S(1)} %get-tuple-element.14.words_all, ...), custom_call_target="tpu_custom_call", output_to_operand_aliasing={{1}: (5, {})} | custom-call | tf_op jit(solution)/shard_map/word_products/pallas_call | solution.py:307
  29.6 52.4 %word_panel_sum.1 = (f32[512,128]{1,0:T(8,128)S(1)}, bf16[8,2,2,4,128,128]{5,4,3,2,1,0:T(8,128)(2,1)S(1)}, f32[32,128,128]{2,1,0:T(8,128)S(1)}) custom-call(f32[8,2,2,512,128]{4,3,2,1,0:T(8,128)S(1)} %bitcast.7), custom_call_target="tpu_custom_call" | custom-call | tf_op jit(solution)/shard_map/word_panel_sum/pallas_call | solution.py:532
  82.0 4.4 %context_products.1 = (f32[32,128,128]{2,1,0:T(8,128)S(1)}, f32[512,128]{1,0:T(8,128)}) custom-call(s32[160]{0:T(256)S(1)} %bitcast.13, s32[160]{0:T(256)S(1)} %bitcast.16, bf16[160,128,128]{2,1,0:T(8,128)(2,1)S(1)} %get-tuple-element.17.tiles, bf16[128,128,128]{2,1,0:T(8,128)(2,1)S(1)} %bitcast.9, ...), custom_call_target="tpu_custom_call", output_to_operand_aliasing={{0}: (5, {})} | custom-call | tf_op jit(solution)/shard_map/context_products/pallas_call | solution.py:567
  86.4 14.6 %context_panel_sum.1 = f32[512,128]{1,0:T(8,128)S(1)} custom-call(f32[2,4,512,128]{3,2,1,0:T(8,128)S(1)} %bitcast.8), custom_call_target="tpu_custom_call" | custom-call | tf_op jit(solution)/shard_map/context_panel_sum/pallas_call | solution.py:597
  101.0 0.7 copy.11
Async XLA Ops:
  0.6 25.1 %copy-start.1 = (s32[1,1,160]{2,1,0:T(1,128)S(1)}, s32[1,1,160]{2,1,0:T(1,128)}, u32[]{:S(2)}) copy-start(s32[1,1,160]{2,1,0:T(1,128)} %param.6) | copy-start | bytes 1924
  0.6 25.1 %copy-start = (s32[1,1,160]{2,1,0:T(1,128)S(1)}, s32[1,1,160]{2,1,0:T(1,128)}, u32[]{:S(2)}) copy-start(s32[1,1,160]{2,1,0:T(1,128)} %param.5) | copy-start | bytes 1924
